TPU v7x, 32 devices: a whole 2x2x4 slice. The times are simulated.
32 devices in a mesh: row: 4 (over z), col: 8 (over y, x, core).
Axes of the slice: x: 2, y: 2, z: 4, core: 2. Of those that a mesh axis runs over, the one named last changes fastest.
Arguments:
- pair_state: bfloat16 [384, 384, 128], P('row', 'col'), may hold values from -40 to 40
- seq_state: bfloat16 [384, 1024], P('row', 'col'), may hold values from -40 to 40
- residue_index: int32 [384], replicated, may hold values from 0 to 1535, as said below
- residue_mask: int32 [384], replicated, may hold values from 0 to 1, as said below
- position_table: bfloat16 [66, 128], replicated, may hold values from -4 to 4
- attention_gain: float32 [2, 1024], replicated, may hold values from 0.1 to 1.9
- bias_norm_gain: float32 [2, 128], replicated, may hold values from 0.1 to 1.9
- query_weight: bfloat16 [2, 1024, 1024], P(None, None, 'col'), may hold values from -16 to 16
- key_weight: bfloat16 [2, 1024, 1024], P(None, None, 'col'), may hold values from -1 to 1
- value_weight: bfloat16 [2, 1024, 1024], P(None, None, 'col'), may hold values from -0.1875 to 0.1875
- gate_weight: bfloat16 [2, 1024, 1024], P(None, None, 'col'), may hold values from -0.1875 to 0.1875
- out_weight: bfloat16 [2, 1024, 1024], P(None, None, 'col'), may hold values from -0.75 to 0.75
- bias_weight: bfloat16 [2, 128, 32], replicated, may hold values from -1.5 to 1.5
- outer_gain: float32 [2, 1024], replicated, may hold values from 0.1 to 1.9
- outer_weight: bfloat16 [2, 1024, 128], replicated, may hold values from -0.1875 to 0.1875
- outer_out_weight: bfloat16 [2, 128, 128], replicated, may hold values from -0.5 to 0.5
- transition_gain: float32 [2, 128], replicated, may hold values from 0.1 to 1.9
- up_weight: bfloat16 [2, 128, 512], replicated, may hold values from -0.5 to 0.5
- down_weight: bfloat16 [2, 512, 128], replicated, may hold values from -0.25 to 0.25
- distance_weight: bfloat16 [128, 64], replicated, may hold values from -0.5 to 0.5
Outputs:
- distogram: bfloat16 [384, 384, 64], P('row', 'col')
- seq_out: bfloat16 [384, 1024], P('row', 'col')
Inputs may be any that keep to these rules, and one draw needn't show every extreme that they name: `residue_index`: strictly increasing; the first entry is 0 and the last is 1535. `residue_mask`: 1 on a prefix of 192 to 383 residues and 0 after it.
All inputs are finite; a program needn't handle non-finite values.
Results may differ from a plain program's by a relative error of at most 0.028.
Values may be sent and summed in bfloat16 or wider, within the bound.
A program may use at most 64 MiB of HBM per device.

v0:
```python
import jax
import jax.numpy as jnp
from jax import lax
from jax.experimental import pallas as pl
from jax.experimental.pallas import tpu as pltpu
from jax.sharding import PartitionSpec as P

HEAD_DIM = 32
RELPOS_MAX = 32
MESH = pl.DeviceIdType.MESH


def normalize(values, weight_gain):
    average = jnp.mean(values, axis=-1, keepdims=True)
    centred = values - average
    spread = jnp.mean(centred * centred, axis=-1, keepdims=True)
    return centred * lax.rsqrt(spread + 1e-05) * weight_gain


def settle(values):
    rounded = lax.optimization_barrier(values.astype(jnp.bfloat16))
    return rounded.astype(jnp.float32)


def gather(block, axis, own_id):
    total = lax.axis_size(axis)

    def kernel(block_ref, out_ref, send_sem, recv_sem, local_sem):
        me = lax.axis_index(axis)
        barrier = pltpu.get_barrier_semaphore()
        for step in range(1, total):
            pl.semaphore_signal(
                barrier, inc=1, device_id={axis: lax.rem(me + step, total)}, device_id_type=MESH
            )
        pl.semaphore_wait(barrier, total - 1)
        copies = []
        for step in range(1, total):
            copies.append(
                pltpu.make_async_remote_copy(
                    src_ref=block_ref,
                    dst_ref=out_ref.at[me],
                    send_sem=send_sem.at[step - 1],
                    recv_sem=recv_sem.at[step - 1],
                    device_id={axis: lax.rem(me + step, total)},
                    device_id_type=MESH,
                )
            )
        for copy in copies:
            copy.start()
        own = pltpu.make_async_copy(block_ref, out_ref.at[me], local_sem)
        own.start()
        own.wait()
        for copy in copies:
            copy.wait()

    return pl.pallas_call(
        kernel,
        out_shape=jax.ShapeDtypeStruct((total,) + block.shape, block.dtype),
        in_specs=[pl.BlockSpec(memory_space=pltpu.VMEM)],
        out_specs=pl.BlockSpec(memory_space=pltpu.VMEM),
        scratch_shapes=[
            pltpu.SemaphoreType.DMA((total - 1,)),
            pltpu.SemaphoreType.DMA((total - 1,)),
            pltpu.SemaphoreType.DMA,
        ],
        compiler_params=pltpu.CompilerParams(collective_id=own_id, has_side_effects=True),
    )(block)


def gather_lanes(block, axis, own_id):
    stacked = gather(block, axis, own_id)
    return jnp.transpose(stacked, (1, 0, 2)).reshape(block.shape[0], -1)


def gather_rows(block, axis, own_id):
    return gather(block, axis, own_id).reshape(-1, block.shape[1])


def mirror(logit_tile, own_id):
    tile_rows, tile_cols, bin_count = logit_tile.shape
    parts = tile_rows // tile_cols
    flat = logit_tile.reshape(parts, tile_cols * tile_cols * bin_count // 128, 128)

    def kernel(flat_ref, out_ref, send_sem, recv_sem, local_sem):
        row, col = lax.axis_index("row"), lax.axis_index("col")
        peer_row, slot = lax.div(col, parts), lax.rem(col, parts)
        barrier = pltpu.get_barrier_semaphore()
        on_diagonal = peer_row == row
        for part in range(parts):
            same = jnp.logical_and(on_diagonal, slot == part)

            @pl.when(jnp.logical_not(same))
            def _(part=part):
                pl.semaphore_signal(
                    barrier,
                    inc=1,
                    device_id={"row": peer_row, "col": row * parts + part},
                    device_id_type=MESH,
                )

        pl.semaphore_wait(barrier, jnp.where(on_diagonal, parts - 1, parts))
        for part in range(parts):
            same = jnp.logical_and(on_diagonal, slot == part)
            away = pltpu.make_async_remote_copy(
                src_ref=flat_ref.at[part],
                dst_ref=out_ref.at[slot],
                send_sem=send_sem.at[part],
                recv_sem=recv_sem.at[slot],
                device_id={"row": peer_row, "col": row * parts + part},
                device_id_type=MESH,
            )
            stay = pltpu.make_async_copy(flat_ref.at[part], out_ref.at[part], local_sem)
            pl.when(jnp.logical_not(same))(away.start)
            pl.when(same)(stay.start)
        for part in range(parts):
            same = jnp.logical_and(on_diagonal, slot == part)
            away = pltpu.make_async_remote_copy(
                src_ref=flat_ref.at[part],
                dst_ref=out_ref.at[part],
                send_sem=send_sem.at[part],
                recv_sem=recv_sem.at[part],
                device_id={"row": peer_row, "col": row * parts + part},
                device_id_type=MESH,
            )
            stay = pltpu.make_async_copy(flat_ref.at[part], out_ref.at[part], local_sem)
            pl.when(jnp.logical_not(same))(away.wait)
            pl.when(same)(stay.wait)

    moved = pl.pallas_call(
        kernel,
        out_shape=jax.ShapeDtypeStruct(flat.shape, flat.dtype),
        in_specs=[pl.BlockSpec(memory_space=pltpu.VMEM)],
        out_specs=pl.BlockSpec(memory_space=pltpu.VMEM),
        scratch_shapes=[
            pltpu.SemaphoreType.DMA((parts,)),
            pltpu.SemaphoreType.DMA((parts,)),
            pltpu.SemaphoreType.DMA,
        ],
        compiler_params=pltpu.CompilerParams(collective_id=own_id, has_side_effects=True),
    )(flat)
    moved = moved.reshape(parts, tile_cols, tile_cols, bin_count)
    return jnp.transpose(moved, (0, 2, 1, 3)).reshape(tile_rows, tile_cols, bin_count)


def per_device(
    pair_state,
    seq_state,
    residue_index,
    residue_mask,
    position_table,
    attention_gain,
    bias_norm_gain,
    query_weight,
    key_weight,
    value_weight,
    gate_weight,
    out_weight,
    bias_weight,
    outer_gain,
    outer_weight,
    outer_out_weight,
    transition_gain,
    up_weight,
    down_weight,
    distance_weight,
):
    col_total = lax.axis_size("col")
    tile_rows, tile_cols, channels = pair_state.shape
    length = tile_cols * col_total
    row_first = lax.axis_index("row") * tile_rows
    col_first = lax.axis_index("col") * tile_cols
    row_pos = lax.dynamic_slice_in_dim(residue_index, row_first, tile_rows)
    col_pos = lax.dynamic_slice_in_dim(residue_index, col_first, tile_cols)
    row_live = lax.dynamic_slice_in_dim(residue_mask, row_first, tile_rows) > 0
    col_live = lax.dynamic_slice_in_dim(residue_mask, col_first, tile_cols) > 0
    key_live = residue_mask > 0
    offset = jnp.clip(col_pos[None, :] - row_pos[:, None], -RELPOS_MAX, RELPOS_MAX) + RELPOS_MAX + 1
    bin_index = jnp.where(row_live[:, None] & col_live[None, :], offset, 0)
    table_rows = position_table.shape[0]
    padded_rows = (table_rows + 127) // 128 * 128
    table_padded = jnp.pad(position_table, ((0, padded_rows - table_rows), (0, 0)))
    one_hot = (
        bin_index.reshape(-1, 1) == jnp.arange(padded_rows, dtype=jnp.int32)[None, :]
    ).astype(jnp.bfloat16)
    pair_now = pair_state.astype(jnp.float32) + jnp.dot(
        one_hot, table_padded, preferred_element_type=jnp.float32
    ).reshape(tile_rows, tile_cols, channels)
    head_width = query_weight.shape[2]
    local_heads = head_width // HEAD_DIM
    score_scale = HEAD_DIM ** (-0.5)
    seq_now = seq_state
    for layer_index in range(query_weight.shape[0]):
        if layer_index == 0:
            seq_full = gather_lanes(seq_now, "col", 0)
        normed_seq = normalize(seq_full.astype(jnp.float32), attention_gain[layer_index]).astype(
            jnp.bfloat16
        )
        queries = (
            jnp.dot(normed_seq, query_weight[layer_index], preferred_element_type=jnp.float32)
            * score_scale
        ).astype(jnp.bfloat16)
        keys_local = jnp.dot(
            normed_seq, key_weight[layer_index], preferred_element_type=jnp.float32
        ).astype(jnp.bfloat16)
        values_local = jnp.dot(
            normed_seq, value_weight[layer_index], preferred_element_type=jnp.float32
        ).astype(jnp.bfloat16)
        gating = jax.nn.sigmoid(
            jnp.dot(normed_seq, gate_weight[layer_index], preferred_element_type=jnp.float32)
        )
        both_all = gather_rows(
            jnp.concatenate([keys_local, values_local], axis=1), "row", 4 * layer_index + 1
        )
        keys_all, values_all = both_all[:, :head_width], both_all[:, head_width:]
        normed_pair = normalize(pair_now, bias_norm_gain[layer_index]).astype(jnp.bfloat16)
        pair_bias = jnp.einsum(
            "ijc,ch->hij", normed_pair, bias_weight[layer_index], preferred_element_type=jnp.float32
        ).astype(jnp.bfloat16)
        head_bias = lax.all_to_all(pair_bias, "col", split_axis=0, concat_axis=2, tiled=True)
        scores = jnp.einsum(
            "qhd,khd->hqk",
            queries.reshape(tile_rows, local_heads, HEAD_DIM),
            keys_all.reshape(length, local_heads, HEAD_DIM),
            preferred_element_type=jnp.float32,
        )
        scores = jnp.where(
            key_live[None, None, :], scores + head_bias.astype(jnp.float32), -jnp.inf
        )
        row_max = jnp.max(scores, axis=-1, keepdims=True)
        shifted = jnp.exp(scores - row_max)
        weights = (shifted / jnp.sum(shifted, axis=-1, keepdims=True)).astype(jnp.bfloat16)
        attended = jnp.einsum(
            "hqk,khd->qhd",
            weights,
            values_all.reshape(length, local_heads, HEAD_DIM),
            preferred_element_type=jnp.float32,
        ).reshape(tile_rows, head_width)
        gated_out = (gating * attended).astype(jnp.bfloat16)
        out_layer = out_weight[layer_index]
        update_seq = jnp.dot(
            gather_lanes(gated_out, "col", 4 * layer_index + 2),
            out_layer,
            preferred_element_type=jnp.float32,
        )
        seq_now = (seq_now.astype(jnp.float32) + update_seq).astype(jnp.bfloat16)
        seq_full = gather_lanes(seq_now, "col", 4 * layer_index + 3)
        outer_in = normalize(seq_full.astype(jnp.float32), outer_gain[layer_index]).astype(
            jnp.bfloat16
        )
        projected = jnp.dot(outer_in, outer_weight[layer_index], preferred_element_type=jnp.float32)
        inner_width = projected.shape[1] // 2
        left_side = projected[:, :inner_width].astype(jnp.bfloat16)
        right_side = projected[:, inner_width:].astype(jnp.bfloat16)
        right_all = gather_rows(right_side, "row", 4 * layer_index + 4)
        right_cols = lax.dynamic_slice_in_dim(right_all, col_first, tile_cols, 0)
        left_wide = left_side.astype(jnp.float32)[:, None, :]
        right_wide = right_cols.astype(jnp.float32)[None, :, :]
        features = jnp.concatenate(
            [left_wide * right_wide, left_wide - right_wide], axis=-1
        ).astype(jnp.bfloat16)
        pair_now = pair_now + jnp.dot(
            features.reshape(-1, 2 * inner_width),
            outer_out_weight[layer_index],
            preferred_element_type=jnp.float32,
        ).reshape(tile_rows, tile_cols, channels)
        normed_pair = normalize(pair_now, transition_gain[layer_index]).astype(jnp.bfloat16)
        hidden = jax.nn.relu(
            jnp.dot(
                normed_pair.reshape(-1, channels),
                up_weight[layer_index],
                preferred_element_type=jnp.float32,
            )
        ).astype(jnp.bfloat16)
        pair_now = settle(
            pair_now
            + jnp.dot(hidden, down_weight[layer_index], preferred_element_type=jnp.float32).reshape(
                tile_rows, tile_cols, channels
            )
        )
    final_pair = pair_now.astype(jnp.bfloat16)
    logits = (
        jnp.dot(
            final_pair.reshape(-1, channels), distance_weight, preferred_element_type=jnp.float32
        )
        .astype(jnp.bfloat16)
        .reshape(tile_rows, tile_cols, distance_weight.shape[1])
    )
    mirrored = mirror(logits, 9)
    distogram = ((logits.astype(jnp.float32) + mirrored.astype(jnp.float32)) * 0.5).astype(
        jnp.bfloat16
    )
    return (distogram, seq_now)


def solution(mesh):
    in_specs = (
        P("row", "col", None),
        P("row", "col"),
        P(),
        P(),
        P(),
        P(),
        P(),
        P(None, None, "col"),
        P(None, None, "col"),
        P(None, None, "col"),
        P(None, None, "col"),
        P(None, None, "col"),
        P(),
        P(),
        P(),
        P(),
        P(),
        P(),
        P(),
        P(),
    )
    out_specs = (P("row", "col", None), P("row", "col"))
    return jax.shard_map(
        per_device, mesh=mesh, in_specs=in_specs, out_specs=out_specs, check_vma=False
    )
```

profile of v0, /device:TPU:3, one launch (start us, length us, event | category | flops | bytes accessed | tf_op | source)
XLA Modules:
  0.0 241.4 jit_solution(9559720409306774514)
XLA Ops:
  4.6 1.5 fusion.7
  6.8 1.4 multiply_reduce_fusion.2
  8.8 3.0 %fusion.10 = bf16[32,96,48]{2,0,1:T(8,128)(2,1)} fusion(f32[128]{0:T(128)S(1)} %get-tuple-element.27, f32[96,48]{1,0:T(8,128)S(1)} %add_rsqrt_fusion.3, f32[96,48]{1,0:T(8,128)S(1)} %broadcast_multiply_fusion.3, f32[96,48,128]{2,1,0:T(8,128)S(1)} %bitcast.203, bf16[96,48,128]{2,1,0:T(8,128)(2,1)S(1)} %copy-done.1, bf16[2,128,32]{1,2,0:T(8,128)(2,1)S(1)} %copy-done.14), kind=kOutput, calls=%fused_computation.34 | convolution fusion | flops 41435136 | bytes 3940864 | tf_op jit(solution)/shard_map/ijc,ch->hij/dot_general | solution.py:216
  11.9 2.6 %copy.61 = bf16[32,96,48]{1,2,0:T(8,128)(2,1)} copy(bf16[32,96,48]{2,0,1:T(8,128)(2,1)} %fusion.10) | data formatting | bytes 589824 | tf_op jit(solution)/shard_map/convert_element_type | solution.py:218
  14.5 4.5 %all-to-all-start = ((bf16[32,96,48]{1,2,0:T(8,128)(2,1)}), bf16[32,96,48]{1,2,0:T(8,128)(2,1)}, u32[]{:S(2)}, u32[]{:S(2)}) async-start(bf16[32,96,48]{1,2,0:T(8,128)(2,1)} %copy.61), calls=%async_computation | async-start | bytes 786432 | tf_op jit(solution)/shard_map/all_to_all | solution.py:219
  20.3 8.2 %shard_map.203 = bf16[8,96,128]{2,1,0:T(8,128)(2,1)} custom-call(bf16[96,128]{1,0:T(8,128)(2,1)} %block_ref.1), custom_call_target="tpu_custom_call" | custom-call | tf_op jit(solution)/shard_map/pallas_call | solution.py:56
  30.8 1.4 fusion.141
  35.5 9.6 %shard_map.204 = bf16[4,96,256]{2,1,0:T(8,128)(2,1)} custom-call(bf16[96,256]{1,0:T(8,128)(2,1)} %pad_maximum_fusion.block_ref), custom_call_target="tpu_custom_call" | custom-call | tf_op jit(solution)/shard_map/pallas_call | solution.py:56
  45.1 1.6 fusion.139
  46.7 1.9 fusion.39
  50.0 1.6 copy.60
  51.6 1.4 copy.59
  53.1 1.6 copy.58
  56.1 1.9 copy.62
  58.0 2.2 copy.63
  60.2 1.4 fusion.12
  63.3 2.7 %fusion.61 = f32[4,32,96]{2,1,0:T(8,128)} fusion(bf16[384,4,32]{0,2,1:T(8,128)(2,1)} %bitcast.222, f32[4,96]{1,0:T(4,128)} %fusion.142, f32[4,96,384]{2,1,0:T(8,128)} %copy-done.3), kind=kOutput, calls=%fused_computation.106 | convolution fusion | flops 9880319 | bytes 738816 | tf_op jit(solution)/shard_map/hqk,khd->qhd/dot_general | solution.py:232
  66.0 1.5 copy.64
  67.6 2.0 fusion.38.block_ref
  69.5 7.4 %shard_map.205 = bf16[8,96,128]{2,1,0:T(8,128)(2,1)} custom-call(bf16[96,128]{1,0:T(8,128)(2,1)} %fusion.38.block_ref), custom_call_target="tpu_custom_call" | custom-call | tf_op jit(solution)/shard_map/pallas_call | solution.py:56
  77.0 1.8 fusion.40.block_ref
  78.8 7.3 %shard_map.206 = bf16[8,96,128]{2,1,0:T(8,128)(2,1)} custom-call(bf16[96,128]{1,0:T(8,128)(2,1)} %fusion.40.block_ref), custom_call_target="tpu_custom_call" | custom-call | tf_op jit(solution)/shard_map/pallas_call | solution.py:56
  89.5 1.8 convolution_convert_fusion.4
  91.3 1.8 convolution_convert_fusion.5
  94.9 6.8 %shard_map.207 = bf16[4,96,64]{2,1,0:T(8,128)(2,1)} custom-call(bf16[96,64]{1,0:T(8,128)(2,1)} %get-tuple-element.19.block_ref), custom_call_target="tpu_custom_call" | custom-call | tf_op jit(solution)/shard_map/pallas_call | solution.py:56
  105.1 1.4 multiply_reduce_fusion.1
  106.6 1.5 multiply_convert_fusion.3
  109.4 1.4 add_convert_fusion.1
  111.5 1.4 fusion.4
  113.0 2.2 fusion.11
  115.3 1.6 copy.71
  116.9 5.0 %all-to-all-start.1 = ((bf16[32,96,48]{1,2,0:T(8,128)(2,1)}), bf16[32,96,48]{1,2,0:T(8,128)(2,1)S(1)}, u32[]{:S(2)}, u32[]{:S(2)}) async-start(bf16[32,96,48]{1,2,0:T(8,128)(2,1)} %copy.71), calls=%async_computation.1 | async-start | bytes 786432 | tf_op jit(solution)/shard_map/all_to_all | solution.py:219
  122.5 8.8 %shard_map.208 = bf16[4,96,256]{2,1,0:T(8,128)(2,1)} custom-call(bf16[96,256]{1,0:T(8,128)(2,1)} %pad_maximum_fusion.1.block_ref), custom_call_target="tpu_custom_call" | custom-call | tf_op jit(solution)/shard_map/pallas_call | solution.py:56
  136.5 7.8 %shard_map.209 = bf16[8,96,128]{2,1,0:T(8,128)(2,1)} custom-call(bf16[96,128]{1,0:T(8,128)(2,1)} %fusion.41.block_ref), custom_call_target="tpu_custom_call" | custom-call | tf_op jit(solution)/shard_map/pallas_call | solution.py:56
  144.3 1.9 fusion.43.block_ref
  146.2 7.3 %shard_map.210 = bf16[8,96,128]{2,1,0:T(8,128)(2,1)} custom-call(bf16[96,128]{1,0:T(8,128)(2,1)} %fusion.43.block_ref), custom_call_target="tpu_custom_call" | custom-call | tf_op jit(solution)/shard_map/pallas_call | solution.py:56
  157.7 6.6 %shard_map.211 = bf16[4,96,64]{2,1,0:T(8,128)(2,1)} custom-call(bf16[96,64]{1,0:T(8,128)(2,1)} %get-tuple-element.17.block_ref), custom_call_target="tpu_custom_call" | custom-call | tf_op jit(solution)/shard_map/pallas_call | solution.py:56
  166.8 1.4 multiply_reduce_fusion
  168.2 1.5 multiply_convert_fusion.1
  171.1 1.4 add_convert_fusion
  175.2 2.3 reshape.435
  177.5 2.5 %reshape_reshape.3.flat_ref = bf16[2,1152,128]{2,1,0:T(8,128)(2,1)} reshape(bf16[4608,64]{1,0:T(8,128)(2,1)} %copy.77) | data formatting | bytes 1179648 | tf_op jit(solution)/shard_map/reshape;reshape | solution.py:82
  180.0 44.5 %shard_map.212 = bf16[2,1152,128]{2,1,0:T(8,128)(2,1)} custom-call(bf16[2,1152,128]{2,1,0:T(8,128)(2,1)} %reshape_reshape.3.flat_ref), custom_call_target="tpu_custom_call" | custom-call | tf_op jit(solution)/shard_map/pallas_call | solution.py:129
  224.5 2.7 %reshape.439 = f32[2,48,48,64]{3,2,1,0:T(8,128)} reshape(bf16[2,1152,128]{2,1,0:T(8,128)(2,1)} %shard_map.212) | data formatting | bytes 1769472 | tf_op jit(solution)/shard_map/convert_element_type | solution.py:289
  227.2 3.8 %copy.78 = f32[2,48,48,64]{3,1,2,0:T(8,128)} copy(f32[2,48,48,64]{3,2,1,0:T(8,128)} %reshape.439) | data formatting | bytes 2359296 | tf_op jit(solution)/shard_map/convert_element_type | solution.py:289
  231.0 3.7 %copy.79 = f32[96,48,64]{1,0,2:T(8,128)} copy(f32[96,48,64]{2,1,0:T(8,128)} %bitcast.207) | data formatting | bytes 2359296 | tf_op jit(solution)/shard_map/convert_element_type | solution.py:289
  234.7 3.7 %multiply_convert_fusion = bf16[96,48,64]{1,0,2:T(8,128)(2,1)} fusion(f32[96,48,64]{1,0,2:T(8,128)S(1)} %reshape.435, f32[96,48,64]{1,0,2:T(8,128)} %copy.79), kind=kLoop, calls=%fused_computation.8 | loop fusion | flops 884736 | bytes 2949120 | tf_op jit(solution)/shard_map/convert_element_type | solution.py:289
  238.4 3.0 %copy.80 = bf16[96,48,64]{0,2,1:T(8,128)(2,1)} copy(bf16[96,48,64]{1,0,2:T(8,128)(2,1)} %multiply_convert_fusion) | data formatting | bytes 1179648
  (116 shorter events, 43.3 us)
Async XLA Ops:
  0.6 171.8 %copy-start = (bf16[128,64]{0,1:T(8,128)(2,1)S(1)}, bf16[128,64]{0,1:T(8,128)(2,1)}, u32[]{:S(2)}) copy-start(bf16[128,64]{0,1:T(8,128)(2,1)} %param.39) | copy-start | bytes 49156
  0.6 5.5 %copy-start.1 = (bf16[96,48,128]{2,1,0:T(8,128)(2,1)S(1)}, bf16[96,48,128]{2,1,0:T(8,128)(2,1)}, u32[]{:S(2)}) copy-start(bf16[96,48,128]{2,1,0:T(8,128)(2,1)} %param.20) | copy-start | bytes 3538948
  6.8 1.5 copy-start.20
  6.8 2.0 copy-start.14
  14.5 41.6 %all-to-all-start = ((bf16[32,96,48]{1,2,0:T(8,128)(2,1)}), bf16[32,96,48]{1,2,0:T(8,128)(2,1)}, u32[]{:S(2)}, u32[]{:S(2)}) async-start(bf16[32,96,48]{1,2,0:T(8,128)(2,1)} %copy.61), calls=%async_computation | async-start | bytes 786432 | tf_op jit(solution)/shard_map/all_to_all | solution.py:219
  29.6 5.2 %copy-start.21 = (f32[96]{0:T(128)}, f32[96]{0:T(128)S(1)}, u32[]{:S(2)}) copy-start(f32[96]{0:T(128)S(1)} %broadcast_multiply_fusion.6) | copy-start | bytes 1156
  30.8 4.1 %copy-start.24 = (f32[96]{0:T(128)}, f32[96]{0:T(128)S(1)}, u32[]{:S(2)}) copy-start(f32[96]{0:T(128)S(1)} %add_rsqrt_fusion.6) | copy-start | bytes 1156
  32.2 1.3 copy-start.17
  61.7 0.8 copy-start.3
  89.5 1.8 copy-start.6
  101.8 1.9 copy-start.8
  105.1 1.5 copy-start.19
  106.5 1.5 copy-start.5
  108.0 1.4 copy-start.4
  110.8 2.2 copy-start.15
  110.8 2.2 copy-start.22
  113.0 8.8 %copy-start.11 = (bf16[96,128]{1,0:T(8,128)(2,1)S(1)}, bf16[96,128]{1,0:T(8,128)(2,1)}, u32[]{:S(2)}) copy-start(bf16[96,128]{1,0:T(8,128)(2,1)} %convolution_convert_fusion.4) | copy-start | bytes 73732
  113.0 8.8 %copy-start.12 = (bf16[96,128]{1,0:T(8,128)(2,1)S(1)}, bf16[96,128]{1,0:T(8,128)(2,1)}, u32[]{:S(2)}) copy-start(bf16[96,128]{1,0:T(8,128)(2,1)} %convolution_convert_fusion.5) | copy-start | bytes 73732
  113.0 19.3 %copy-start.7 = (bf16[8,12,8,128]{3,2,1,0:T(8,128)(2,1)S(1)}, bf16[8,12,8,128]{3,2,1,0:T(8,128)(2,1)}, u32[]{:S(2)}) copy-start(bf16[8,12,8,128]{3,2,1,0:T(8,128)(2,1)} %copy-done.6) | copy-start | bytes 589828
  116.9 16.9 %all-to-all-start.1 = ((bf16[32,96,48]{1,2,0:T(8,128)(2,1)}), bf16[32,96,48]{1,2,0:T(8,128)(2,1)S(1)}, u32[]{:S(2)}, u32[]{:S(2)}) async-start(bf16[32,96,48]{1,2,0:T(8,128)(2,1)} %copy.71), calls=%async_computation.1 | async-start | bytes 786432 | tf_op jit(solution)/shard_map/all_to_all | solution.py:219
  121.8 12.3 %copy-start.13 = (pred[384]{0:T(512)(128)(4,1)S(1)}, pred[384]{0:T(512)(128)(4,1)}, u32[]{:S(2)}) copy-start(pred[384]{0:T(512)(128)(4,1)} %broadcast_compare_fusion) | copy-start | bytes 1156
  134.4 1.2 copy-start.23
  134.4 9.8 %copy-start.10 = (bf16[96,128]{1,0:T(8,128)(2,1)S(1)}, bf16[96,128]{1,0:T(8,128)(2,1)}, u32[]{:S(2)}) copy-start(bf16[96,128]{1,0:T(8,128)(2,1)} %fusion.40.block_ref) | copy-start | bytes 73732
  134.7 21.0 %copy-start.16 = (f32[1,1024]{1,0:T(1,128)S(1)}, f32[1,1024]{1,0:T(1,128)}, u32[]{:S(2)}) copy-start(f32[1,1024]{1,0:T(1,128)} %get-tuple-element.20) | copy-start | bytes 12292
  144.3 21.2 %copy-start.9 = (bf16[2,128,128]{2,1,0:T(8,128)(2,1)S(1)}, bf16[2,128,128]{2,1,0:T(8,128)(2,1)}, u32[]{:S(2)}) copy-start(bf16[2,128,128]{2,1,0:T(8,128)(2,1)} %param.35) | copy-start | bytes 196612
  166.7 1.5 copy-start.18
  173.0 0.8 copy-start.2
where the time goes:
time: 244 us; the launch traced here: 241 us
  Pallas kernels  114 us (47%)
  local copies, waits for them, and re-layouts  45.9 us (19%)
  matrix products  38.9 us (16%)
  other arithmetic  31.3 us (13%)
  starting transfers between devices  9.5 us (4%)
    pallas_call x9, Pallas kernels, gather(): pl.pallas_call(kernel, out_shape=jax.ShapeDtypeStruct((total,) + block.sh...  69.9 us
    pallas_call x1, Pallas kernels, mirror(): pl.pallas_call(kernel, out_shape=jax.ShapeDtypeStruct(flat.shape, flat.dt...  44.5 us
    convert_element_type x3, local copies, waits for them, and re-layouts, per_device(): mirrored.astype(jnp.float32)  10.2 us
    all_to_all x2, starting transfers between devices, per_device(): lax.all_to_all(pair_bias, 'col', split_axis=0, concat_axis=2, tiled=True)  9.5 us
    reduce_sum x7, other arithmetic, normalize(): spread = jnp.mean(centred * centred, axis=-1, keepdims=True)  9.12 us
    slice x6, local copies, waits for them, and re-layouts, per_device(): keys_all, values_all = (both_all[:, :head_width], both_all[:, head_width:])  6.09 us
    dot_general x2, matrix products, per_device(): jnp.einsum('ijc,ch->hij', normed_pair, bias_weight[layer_index], preferre...  5.27 us
  transfers between devices with their start and end apart: 2, of which 0 were waited for; matrix products, arithmetic and copies ran while one was open for 9% of the time, Pallas kernels for 11%

commit v1 on v0

v1 whole, which is shorter than its diff:
```python
import jax
import jax.numpy as jnp
from jax import lax
from jax.experimental import pallas as pl
from jax.experimental.pallas import tpu as pltpu
from jax.sharding import PartitionSpec as P

HEAD_DIM = 32
RELPOS_MAX = 32
MESH = pl.DeviceIdType.MESH


def normalize(values, weight_gain):
    average = jnp.mean(values, axis=-1, keepdims=True)
    centred = values - average
    spread = jnp.mean(centred * centred, axis=-1, keepdims=True)
    return centred * lax.rsqrt(spread + 1e-05) * weight_gain


def full_spec():
    return pl.BlockSpec(memory_space=pltpu.VMEM)


def lane_join(stacked_ref):
    return jnp.concatenate([stacked_ref[k] for k in range(stacked_ref.shape[0])], axis=1)


def spread(source, target, axis, send_sem, recv_sem):
    total, me = lax.axis_size(axis), lax.axis_index(axis)
    copies = []
    for step in range(1, total):
        peer = lax.rem(me + step, total)
        copies.append(
            pltpu.make_async_remote_copy(
                src_ref=source(peer),
                dst_ref=target(me),
                send_sem=send_sem.at[step - 1],
                recv_sem=recv_sem.at[step - 1],
                device_id={axis: peer},
                device_id_type=MESH,
            )
        )
    for copy in copies:
        copy.start()
    return copies


def finish(copies):
    for copy in copies:
        copy.wait()


def sequence_step(
    layer, seq_tile, seq_all, bias_send, live_column, gains, weights, outer_weight, own_id
):
    nr, nc = lax.axis_size("row"), lax.axis_size("col")
    tr, width = seq_tile.shape
    heads, tc, lanes = bias_send.shape
    hl = heads // nc
    length = nr * tr
    cs = outer_weight.shape[1]
    wide = outer_weight.shape[2]
    first = seq_all is None
    score_scale = HEAD_DIM ** (-0.5)

    def kernel(*refs):
        it = iter(refs)
        seq_ref = next(it)
        seq_all_ref = None if first else next(it)
        bias_ref, live_ref, gain_ref, outer_gain_ref = (next(it) for _ in range(4))
        weight_hbm = [next(it) for _ in range(6)]
        seq_out, seq_out_all, proj_all = (next(it) for _ in range(3))
        weight_refs = [next(it) for _ in range(6)]
        gathered, kv_all, bias_all, gated_all = (next(it) for _ in range(4))
        weight_sem = next(it)
        col_send, col_recv, row_send, row_recv = (next(it) for _ in range(4))

        loads = [
            pltpu.make_async_copy(weight_hbm[k].at[layer], weight_refs[k], weight_sem.at[k])
            for k in range(6)
        ]
        for load in loads:
            load.start()
        row, col = lax.axis_index("row"), lax.axis_index("col")
        barrier = pltpu.get_barrier_semaphore()
        for axis, total, me in (("col", nc, col), ("row", nr, row)):
            for step in range(1, total):
                pl.semaphore_signal(
                    barrier,
                    inc=1,
                    device_id={axis: lax.rem(me + step, total)},
                    device_id_type=MESH,
                )
        pl.semaphore_wait(barrier, nc + nr - 2)
        if first:
            seq_copies = spread(
                lambda peer: seq_ref,
                lambda me: gathered.at[me],
                "col",
                col_send.at[0],
                col_recv.at[0],
            )
        bias_copies = spread(
            lambda peer: bias_ref.at[pl.ds(peer * hl, hl)],
            lambda me: bias_all.at[me],
            "col",
            col_send.at[1],
            col_recv.at[1],
        )
        bias_all[col] = bias_ref[pl.ds(col * hl, hl)]
        if first:
            gathered[col] = seq_ref[...]
            finish(seq_copies)
            entering = lane_join(gathered)
        else:
            entering = lane_join(seq_all_ref)
        normed = normalize(entering.astype(jnp.float32), gain_ref[pl.ds(layer, 1), :]).astype(
            jnp.bfloat16
        )

        def product(value, k):
            return jnp.dot(value, weight_refs[k][...], preferred_element_type=jnp.float32)

        loads[1].wait()
        kv_all[row, 0] = product(normed, 1).astype(jnp.bfloat16)
        loads[2].wait()
        kv_all[row, 1] = product(normed, 2).astype(jnp.bfloat16)
        kv_copies = spread(
            lambda peer: kv_all.at[row],
            lambda me: kv_all.at[me],
            "row",
            row_send.at[0],
            row_recv.at[0],
        )
        loads[0].wait()
        queries = (product(normed, 0) * score_scale).astype(jnp.bfloat16)
        loads[3].wait()
        gating = jax.nn.sigmoid(product(normed, 3))
        head_of = lax.broadcasted_iota(jnp.int32, (tr, width), 1) // HEAD_DIM
        finish(kv_copies)
        finish(bias_copies)
        keys = kv_all[:, 0].reshape(length, width)
        values = kv_all[:, 1].reshape(length, width)
        live = live_ref[...] > 0
        attended = jnp.zeros((tr, width), jnp.float32)
        for head in range(hl):
            own = head_of == head
            query = jnp.where(own, queries.astype(jnp.float32), 0.0).astype(jnp.bfloat16)
            scores = lax.dot_general(
                keys, query, (((1,), (1,)), ((), ())), preferred_element_type=jnp.float32
            )
            bias = bias_all[:, head].reshape(length, lanes)[:, :tr]
            scores = jnp.where(live, scores + bias.astype(jnp.float32), -jnp.inf)
            shifted = jnp.exp(scores - jnp.max(scores, axis=0, keepdims=True))
            share = (shifted / jnp.sum(shifted, axis=0, keepdims=True)).astype(jnp.bfloat16)
            mixed = lax.dot_general(
                share, values, (((0,), (0,)), ((), ())), preferred_element_type=jnp.float32
            )
            attended = jnp.where(own, mixed, attended)
        gated_all[col] = (gating * attended).astype(jnp.bfloat16)
        finish(
            spread(
                lambda peer: gated_all.at[col],
                lambda me: gated_all.at[me],
                "col",
                col_send.at[2],
                col_recv.at[2],
            )
        )
        loads[4].wait()
        leaving = (seq_ref[...].astype(jnp.float32) + product(lane_join(gated_all), 4)).astype(
            jnp.bfloat16
        )
        seq_out_all[col] = leaving
        seq_out[...] = leaving
        finish(
            spread(
                lambda peer: seq_out_all.at[col],
                lambda me: seq_out_all.at[me],
                "col",
                col_send.at[3],
                col_recv.at[3],
            )
        )
        outer_in = normalize(
            lane_join(seq_out_all).astype(jnp.float32), outer_gain_ref[pl.ds(layer, 1), :]
        ).astype(jnp.bfloat16)
        loads[5].wait()
        proj_all[row] = product(outer_in, 5).astype(jnp.bfloat16)
        finish(
            spread(
                lambda peer: proj_all.at[row],
                lambda me: proj_all.at[me],
                "row",
                row_send.at[1],
                row_recv.at[1],
            )
        )

    operands = [seq_tile] + ([] if first else [seq_all]) + [bias_send, live_column, *gains]
    specs = [full_spec()] * len(operands) + [pl.BlockSpec(memory_space=pl.ANY)] * 6
    bf16 = jnp.bfloat16
    return pl.pallas_call(
        kernel,
        out_shape=(
            jax.ShapeDtypeStruct((tr, width), bf16),
            jax.ShapeDtypeStruct((nc, tr, width), bf16),
            jax.ShapeDtypeStruct((nr, tr, wide), bf16),
        ),
        in_specs=specs,
        out_specs=(full_spec(),) * 3,
        scratch_shapes=[pltpu.VMEM((cs, width), bf16)] * 5
        + [
            pltpu.VMEM((cs, wide), bf16),
            pltpu.VMEM((nc, tr, width), bf16),
            pltpu.VMEM((nr, 2, tr, width), bf16),
            pltpu.VMEM((nc, hl, tc, lanes), bf16),
            pltpu.VMEM((nc, tr, width), bf16),
            pltpu.SemaphoreType.DMA((6,)),
            pltpu.SemaphoreType.DMA((4, nc - 1)),
            pltpu.SemaphoreType.DMA((4, nc - 1)),
            pltpu.SemaphoreType.DMA((2, nr - 1)),
            pltpu.SemaphoreType.DMA((2, nr - 1)),
        ],
        compiler_params=pltpu.CompilerParams(collective_id=own_id, has_side_effects=True),
    )(*operands, *weights, outer_weight)


def bias_rows(pair_ref, gain, weight, mixed_ref, out_ref, tr, tc):
    heads = weight.shape[0]

    @pl.loop(0, tc, unroll=4)
    def _(j):
        normed = normalize(pair_ref[pl.ds(j, tr, stride=tc), :], gain).astype(jnp.bfloat16)
        mixed_ref[pl.ds(j * heads, heads), 0:tr] = lax.dot_general(
            weight, normed, (((1,), (1,)), ((), ())), preferred_element_type=jnp.float32
        )

    for head in range(heads):
        out_ref[head] = mixed_ref[pl.ds(head, tc, stride=heads), :].astype(jnp.bfloat16)


def bias_step(layer, pair_flat, tr, tc, bias_norm_gain, bias_weight_t):
    heads = bias_weight_t.shape[1]
    lanes = (tr + 127) // 128 * 128

    def kernel(pair_ref, gain_ref, weight_ref, out_ref, mixed_ref):
        bias_rows(pair_ref, gain_ref[pl.ds(layer, 1), :], weight_ref[layer], mixed_ref, out_ref, tr, tc)

    return pl.pallas_call(
        kernel,
        out_shape=jax.ShapeDtypeStruct((heads, tc, lanes), jnp.bfloat16),
        in_specs=[full_spec()] * 3,
        out_specs=full_spec(),
        scratch_shapes=[pltpu.VMEM((tc * heads, lanes), jnp.float32)],
    )(pair_flat, bias_norm_gain, bias_weight_t)


def pair_step(layer, last, pair_flat, proj_all, tr, tc, mats, gains, bias_weight_t, heads_of_bins):
    channels = pair_flat.shape[1]
    heads = bias_weight_t.shape[1]
    lanes = (tr + 127) // 128 * 128
    rows = 8
    parts = tr // tc
    half = tc // 2

    def kernel(
        pair_ref,
        proj_ref,
        outer_ref,
        up_ref,
        down_ref,
        transition_ref,
        bias_gain_ref,
        bias_weight_ref,
        bins_ref,
        out_ref,
        extra_ref,
        fresh_ref,
        mixed_ref,
        left_ref,
    ):
        row, col = lax.axis_index("row"), lax.axis_index("col")
        low = lax.broadcasted_iota(jnp.int32, (1, channels), 1) < channels // 2
        left = proj_ref[pl.ds(pl.multiple_of(row * tr, 16), tr), :].astype(jnp.float32)
        left_ref[...] = jnp.where(low, left, pltpu.roll(left, channels // 2, axis=1))
        right = proj_ref[pl.ds(pl.multiple_of(col * tc, 16), tc), :].astype(jnp.float32)
        right = jnp.where(low, pltpu.roll(right, channels // 2, axis=1), right)[None]
        gain = transition_ref[pl.ds(layer, 1), :]

        @pl.loop(0, tr // rows)
        def _(step):
            at = pl.ds(pl.multiple_of(step * (rows * tc), rows * tc), rows * tc)
            left = left_ref[pl.ds(pl.multiple_of(step * rows, rows), rows), :][:, None, :]
            features = jnp.where(low[None], left * right, left - right)
            features = features.reshape(rows * tc, channels).astype(jnp.bfloat16)
            middle = pair_ref[at, :].astype(jnp.float32) + jnp.dot(
                features, outer_ref[layer], preferred_element_type=jnp.float32
            )
            normed = normalize(middle, gain).astype(jnp.bfloat16)
            hidden = jnp.maximum(
                jnp.dot(normed, up_ref[layer], preferred_element_type=jnp.float32), 0.0
            ).astype(jnp.bfloat16)
            fresh = (
                middle + jnp.dot(hidden, down_ref[layer], preferred_element_type=jnp.float32)
            ).astype(jnp.bfloat16)
            if last:
                fresh_ref[at, :] = fresh.astype(jnp.float32)
                out_ref[at, :] = jnp.dot(
                    fresh, bins_ref[0], preferred_element_type=jnp.float32
                ).astype(jnp.bfloat16)
            else:
                out_ref[at, :] = fresh
                fresh_ref[at, :] = fresh.astype(jnp.float32)

        if last:
            count = half * tc
            for part in range(parts):
                near = fresh_ref[pl.ds(part * 2 * count, count), :].astype(jnp.bfloat16)
                far = fresh_ref[pl.ds((part * 2 + 1) * count, count), :].astype(jnp.bfloat16)
                extra_ref[part] = (
                    jnp.dot(near, bins_ref[0], preferred_element_type=jnp.float32)
                    + jnp.dot(far, bins_ref[1], preferred_element_type=jnp.float32)
                ).astype(jnp.bfloat16)
        else:
            bias_rows(
                fresh_ref,
                bias_gain_ref[pl.ds(layer + 1, 1), :],
                bias_weight_ref[layer + 1],
                mixed_ref,
                extra_ref,
                tr,
                tc,
            )

    width = heads_of_bins.shape[2]
    extra = (parts, half * tc, width) if last else (heads, tc, lanes)
    operands = (pair_flat, proj_all, *mats, *gains, bias_weight_t, heads_of_bins)
    return pl.pallas_call(
        kernel,
        out_shape=(
            jax.ShapeDtypeStruct((tr * tc, width if last else channels), jnp.bfloat16),
            jax.ShapeDtypeStruct(extra, jnp.bfloat16),
        ),
        in_specs=[full_spec()] * len(operands),
        out_specs=(full_spec(),) * 2,
        scratch_shapes=[
            pltpu.VMEM((tr * tc, channels), jnp.float32),
            pltpu.VMEM((tc * heads, lanes), jnp.float32),
            pltpu.VMEM((tr, channels), jnp.float32),
        ],
    )(*operands)


def mirror(logit_flat, flat, tile_rows, tile_cols, bin_count, own_id):
    parts = tile_rows // tile_cols
    half = tile_cols // 2

    def kernel(flat_ref, logit_ref, final_ref, out_ref, wide_ref, send_sem, recv_sem, local_sem):
        row, col = lax.axis_index("row"), lax.axis_index("col")
        peer_row, slot = lax.div(col, parts), lax.rem(col, parts)
        barrier = pltpu.get_barrier_semaphore()
        on_diagonal = peer_row == row
        for part in range(parts):
            same = jnp.logical_and(on_diagonal, slot == part)

            @pl.when(jnp.logical_not(same))
            def _(part=part):
                pl.semaphore_signal(
                    barrier,
                    inc=1,
                    device_id={"row": peer_row, "col": row * parts + part},
                    device_id_type=MESH,
                )

        pl.semaphore_wait(barrier, jnp.where(on_diagonal, parts - 1, parts))
        for part in range(parts):
            same = jnp.logical_and(on_diagonal, slot == part)
            away = pltpu.make_async_remote_copy(
                src_ref=flat_ref.at[part],
                dst_ref=out_ref.at[slot],
                send_sem=send_sem.at[part],
                recv_sem=recv_sem.at[slot],
                device_id={"row": peer_row, "col": row * parts + part},
                device_id_type=MESH,
            )
            stay = pltpu.make_async_copy(flat_ref.at[part], out_ref.at[part], local_sem)
            pl.when(jnp.logical_not(same))(away.start)
            pl.when(same)(stay.start)
        for part in range(parts):
            same = jnp.logical_and(on_diagonal, slot == part)
            away = pltpu.make_async_remote_copy(
                src_ref=flat_ref.at[part],
                dst_ref=out_ref.at[part],
                send_sem=send_sem.at[part],
                recv_sem=recv_sem.at[part],
                device_id={"row": peer_row, "col": row * parts + part},
                device_id_type=MESH,
            )
            stay = pltpu.make_async_copy(flat_ref.at[part], out_ref.at[part], local_sem)
            pl.when(jnp.logical_not(same))(away.wait)
            pl.when(same)(stay.wait)
        for part in range(parts):
            wide_ref[...] = out_ref[part].astype(jnp.float32)

            @pl.loop(0, tile_cols, unroll=4)
            def _(i, part=part):
                packed = wide_ref[pl.ds(i, half, stride=tile_cols), :]
                other = pltpu.roll(packed, packed.shape[1] - bin_count, axis=1)
                flipped = jnp.concatenate([packed, other], axis=0)
                at = pl.multiple_of((part * tile_cols + i) * tile_cols, 16)
                own = logit_ref[pl.ds(at, tile_cols), :].astype(jnp.float32)
                final = ((own + flipped) * 0.5).astype(jnp.bfloat16)
                final_ref[part * tile_cols + i] = final[:, :bin_count]

    width = flat.shape[2]
    return pl.pallas_call(
        kernel,
        out_shape=jax.ShapeDtypeStruct((tile_rows, tile_cols, bin_count), jnp.bfloat16),
        in_specs=[full_spec()] * 2,
        out_specs=full_spec(),
        scratch_shapes=[
            pltpu.VMEM(flat.shape, flat.dtype),
            pltpu.VMEM((half * tile_cols, width), jnp.float32),
            pltpu.SemaphoreType.DMA((parts,)),
            pltpu.SemaphoreType.DMA((parts,)),
            pltpu.SemaphoreType.DMA,
        ],
        compiler_params=pltpu.CompilerParams(collective_id=own_id, has_side_effects=True),
    )(flat, logit_flat)


def per_device(
    pair_state,
    seq_state,
    residue_index,
    residue_mask,
    position_table,
    attention_gain,
    bias_norm_gain,
    query_weight,
    key_weight,
    value_weight,
    gate_weight,
    out_weight,
    bias_weight,
    outer_gain,
    outer_weight,
    outer_out_weight,
    transition_gain,
    up_weight,
    down_weight,
    distance_weight,
):
    col_total = lax.axis_size("col")
    tile_rows, tile_cols, channels = pair_state.shape
    length = tile_cols * col_total
    row_first = lax.axis_index("row") * tile_rows
    col_first = lax.axis_index("col") * tile_cols
    row_pos = lax.dynamic_slice_in_dim(residue_index, row_first, tile_rows)
    col_pos = lax.dynamic_slice_in_dim(residue_index, col_first, tile_cols)
    row_live = lax.dynamic_slice_in_dim(residue_mask, row_first, tile_rows) > 0
    col_live = lax.dynamic_slice_in_dim(residue_mask, col_first, tile_cols) > 0
    offset = jnp.clip(col_pos[None, :] - row_pos[:, None], -RELPOS_MAX, RELPOS_MAX) + RELPOS_MAX + 1
    bin_index = jnp.where(row_live[:, None] & col_live[None, :], offset, 0)
    table_rows = position_table.shape[0]
    padded_rows = (table_rows + 127) // 128 * 128
    table_padded = jnp.pad(position_table, ((0, padded_rows - table_rows), (0, 0)))
    one_hot = (
        bin_index.reshape(-1, 1) == jnp.arange(padded_rows, dtype=jnp.int32)[None, :]
    ).astype(jnp.bfloat16)
    pair_now = pair_state.astype(jnp.float32) + jnp.dot(
        one_hot, table_padded, preferred_element_type=jnp.float32
    ).reshape(tile_rows, tile_cols, channels)
    pair_flat = pair_now.reshape(-1, channels)
    bias_weight_t = jnp.swapaxes(bias_weight, 1, 2)
    live_column = residue_mask.reshape(-1, 1)
    bin_count = distance_weight.shape[1]
    bins_pair = jnp.stack(
        [
            jnp.pad(distance_weight, ((0, 0), (0, bin_count))),
            jnp.pad(distance_weight, ((0, 0), (bin_count, 0))),
        ]
    )
    layers = query_weight.shape[0]
    extra = bias_step(0, pair_flat, tile_rows, tile_cols, bias_norm_gain, bias_weight_t)
    seq_now, seq_all = seq_state, None
    for layer in range(layers):
        seq_now, seq_all, proj_all = sequence_step(
            layer,
            seq_now,
            seq_all,
            extra,
            live_column,
            (attention_gain, outer_gain),
            (query_weight, key_weight, value_weight, gate_weight, out_weight),
            outer_weight,
            layer,
        )
        pair_flat, extra = pair_step(
            layer,
            layer == layers - 1,
            pair_flat,
            proj_all.reshape(-1, proj_all.shape[2]),
            tile_rows,
            tile_cols,
            (outer_out_weight, up_weight, down_weight),
            (transition_gain, bias_norm_gain),
            bias_weight_t,
            bins_pair,
        )
    distogram = mirror(pair_flat, extra, tile_rows, tile_cols, bin_count, layers)
    return (distogram, seq_now)


def solution(mesh):
    in_specs = (
        P("row", "col", None),
        P("row", "col"),
        P(),
        P(),
        P(),
        P(),
        P(),
        P(None, None, "col"),
        P(None, None, "col"),
        P(None, None, "col"),
        P(None, None, "col"),
        P(None, None, "col"),
        P(),
        P(),
        P(),
        P(),
        P(),
        P(),
        P(),
        P(),
    )
    out_specs = (P("row", "col", None), P("row", "col"))
    return jax.shard_map(
        per_device, mesh=mesh, in_specs=in_specs, out_specs=out_specs, check_vma=False
    )
```

time: 244 us -> 151 us (0.62); the launches traced: 241 us -> 151 us
  local copies, waits for them, and re-layouts: 45.9 us -> 5.66 us
  matrix products: 38.9 us -> 1.51 us
  other arithmetic: 31.3 us -> 4.09 us
  Pallas kernels: 114 us -> 139 us
  starting transfers between devices: 9.5 us -> 0 us
    dot_general x25 -> x0, matrix products: 37.4 us -> none  [the longest x2 5.27 us: per_device(): jnp.einsum('ijc,ch->hij', normed_pair, bias_weight[layer_index], preferre...]
    pallas_call x10 -> x6, Pallas kernels: 114 us -> 139 us  [the longest x2 55.1 us: sequence_step(): pl.pallas_call(kernel, out_shape=(jax.ShapeDtypeStruct((tr, width), bf16)...]
    convert_element_type x13 -> x0, local copies, waits for them, and re-layouts: 24.1 us -> none  [the longest x3 10.2 us: per_device(): mirrored.astype(jnp.float32)]
    reduce_sum x12 -> x0, other arithmetic: 13.6 us -> none  [the longest x7 9.12 us: normalize(): spread = jnp.mean(centred * centred, axis=-1, keepdims=True)]
    all_to_all x2 -> x0, starting transfers between devices: 9.5 us -> none  [per_device(): lax.all_to_all(pair_bias, 'col', split_axis=0, concat_axis=2, tiled=True)]
    convert_element_type x7 -> x0, other arithmetic: 9.44 us -> none  [the longest x1 3.66 us: per_device(): ((logits.astype(jnp.float32) + mirrored.astype(jnp.float32)) * 0.5).astyp...]
    slice x8 -> x0, local copies, waits for them, and re-layouts: 8.84 us -> none  [the longest x6 6.09 us: per_device(): keys_all, values_all = (both_all[:, :head_width], both_all[:, head_width:])]
  transfers between devices with their start and end apart: 2 -> 0, of which waited for: 0 -> 0; matrix products, arithmetic and copies ran while one was open for 9% -> 0% of each run, Pallas kernels for 11% -> 0%
where the time goes in v1:
time: 151 us
  Pallas kernels  139 us (92%)
  local copies, waits for them, and re-layouts  5.66 us (4%)
  other arithmetic  4.09 us (3%)
  matrix products  1.51 us (1%)
    pallas_call x2, Pallas kernels, sequence_step(): pl.pallas_call(kernel, out_shape=(jax.ShapeDtypeStruct((tr, width), bf16)...  55.1 us
    pallas_call x1, Pallas kernels, mirror(): pl.pallas_call(kernel, out_shape=jax.ShapeDtypeStruct((tile_rows, tile_co...  47.4 us
    pallas_call x2, Pallas kernels, pair_step(): pl.pallas_call(kernel, out_shape=(jax.ShapeDtypeStruct((tr * tc, width if...  29.5 us
    pallas_call x1, Pallas kernels, bias_step(): pl.pallas_call(kernel, out_shape=jax.ShapeDtypeStruct((heads, tc, lanes),...  6.94 us
    unnamed x11, local copies, waits for them, and re-layouts  3.19 us

profile of v1, /device:TPU:3, one launch (start us, length us, event | category | flops | bytes accessed | tf_op | source)
XLA Modules:
  0.0 151.0 jit_solution(4249399241136460260)
XLA Ops:
  0.6 0.0 copy-start
  0.6 0.9 dynamic-slice_compare_fusion
  1.5 0.8 dynamic_slice.14
  2.3 0.8 dynamic-slice_compare_fusion.1
  3.0 0.8 dynamic_slice.15
  3.8 0.1 add_select_fusion
  3.9 0.1 select_n.22
  4.0 1.5 %fusion = f32[4608,128]{1,0:T(8,128)S(1)} fusion(s32[4608]{0:T(1024)S(1)} %select_n.22, bf16[66,128]{1,0:T(8,128)(2,1)} %param.24), kind=kOutput, calls=%fused_computation.2 | convolution fusion | flops 151584768 | bytes 2394624 | tf_op jit(solution)/shard_map/dot_general | solution.py:472
  5.5 0.0 copy-done
  5.5 1.7 %convert_add_fusion = f32[96,48,128]{2,1,0:T(8,128)} fusion(f32[96,48,128]{2,1,0:T(8,128)S(1)} %bitcast.11, bf16[96,48,128]{2,1,0:T(8,128)(2,1)S(1)} %copy-done), kind=kLoop, calls=%fused_computation.1 | loop fusion | flops 1179648 | bytes 5898240 | tf_op jit(solution)/shard_map/add | solution.py:472
  7.2 0.0 copy-start.3
  7.2 6.9 %shard_map.203.refs_1_ = bf16[32,48,128]{2,1,0:T(8,128)(2,1)} custom-call(f32[4608,128]{1,0:T(8,128)} %bitcast.9, f32[2,128]{1,0:T(2,128)} %bias_gain_ref.3, bf16[2,32,128]{2,1,0:T(8,128)(2,1)} %bitcast.12), custom_call_target="tpu_custom_call" | custom-call | tf_op jit(solution)/shard_map/pallas_call | solution.py:250
  14.2 0.0 copy-done.3
  14.2 0.0 copy-start.2
  14.2 0.8 reshape.67.refs_2_.refs_3_
  15.0 30.8 %shard_map.204 = (bf16[96,128]{1,0:T(8,128)(2,1)}, bf16[8,96,128]{2,1,0:T(8,128)(2,1)}, bf16[4,96,128]{2,1,0:T(8,128)(2,1)}) custom-call(bf16[96,128]{1,0:T(8,128)(2,1)} %refs_0_.1, bf16[32,48,128]{2,1,0:T(8,128)(2,1)} %shard_map.203.refs_1_, s32[384,1]{1,0:T(8,128)} %reshape.67.refs_2_.refs_3_, f32[2,1024]{1,0:T(2,128)} %refs_4_.3, f32[2,1024]{1,0:T(2,128)} %refs_5_.3, ...), custom_call_target="tpu_custom_call" | custom-call | tf_op jit(solution)/shard_map/pallas_call | solution.py:203
  45.8 0.0 copy-done.2
  45.8 0.1 copy.26
  45.9 0.1 pad_bitcast_fusion.1
  46.0 0.7 pad_maximum_fusion.bins_ref
  46.7 16.3 %shard_map.205 = (bf16[4608,128]{1,0:T(8,128)(2,1)}, bf16[32,48,128]{2,1,0:T(8,128)(2,1)}) custom-call(f32[4608,128]{1,0:T(8,128)} %bitcast.10, bf16[384,128]{1,0:T(8,128)(2,1)} %bitcast.15, bf16[2,128,128]{2,1,0:T(8,128)(2,1)} %outer_ref.3, bf16[2,128,512]{2,1,0:T(8,128)(2,1)} %up_ref.3, bf16[2,512,128]{2,1,0:T(8,128)(2,1)} %down_ref.3, ...), custom_call_target="tpu_custom_call" | custom-call | tf_op jit(solution)/shard_map/pallas_call | solution.py:339
  63.0 24.3 %shard_map.206 = (bf16[96,128]{1,0:T(8,128)(2,1)}, bf16[8,96,128]{2,1,0:T(8,128)(2,1)}, bf16[4,96,128]{2,1,0:T(8,128)(2,1)}) custom-call(bf16[96,128]{1,0:T(8,128)(2,1)} %get-tuple-element.13.refs_0_, bf16[8,96,128]{2,1,0:T(8,128)(2,1)} %get-tuple-element.14.refs_1_, bf16[32,48,128]{2,1,0:T(8,128)(2,1)} %get-tuple-element.15.refs_2_, ...), custom_call_target="tpu_custom_call" | custom-call | tf_op jit(solution)/shard_map/pallas_call | solution.py:203
  87.3 13.2 %shard_map.207 = (bf16[4608,128]{1,0:T(8,128)(2,1)}, bf16[2,1152,128]{2,1,0:T(8,128)(2,1)}) custom-call(bf16[4608,128]{1,0:T(8,128)(2,1)} %get-tuple-element.12.pair_ref, bf16[384,128]{1,0:T(8,128)(2,1)} %bitcast.16, bf16[2,128,128]{2,1,0:T(8,128)(2,1)} %outer_ref.3, bf16[2,128,512]{2,1,0:T(8,128)(2,1)} %up_ref.3, bf16[2,512,128]{2,1,0:T(8,128)(2,1)} %down_ref.3, ...), custom_call_target="tpu_custom_call" | custom-call | tf_op jit(solution)/shard_map/pallas_call | solution.py:339
  100.5 0.0 copy-start.1
  100.5 47.4 %shard_map.208 = bf16[96,48,64]{2,1,0:T(8,128)(2,1)} custom-call(bf16[2,1152,128]{2,1,0:T(8,128)(2,1)} %get-tuple-element.17.flat_ref, bf16[4608,128]{1,0:T(8,128)(2,1)} %get-tuple-element.18.logit_ref), custom_call_target="tpu_custom_call" | custom-call | tf_op jit(solution)/shard_map/pallas_call | solution.py:417
  147.9 2.4 %copy.29 = bf16[96,48,64]{0,2,1:T(8,128)(2,1)} copy(bf16[96,48,64]{2,1,0:T(8,128)(2,1)} %shard_map.208) | data formatting | bytes 1179648
  150.3 0.0 copy-done.1
  150.3 0.6 copy.31
Async XLA Ops:
  0.6 4.8 %copy-start = (bf16[96,48,128]{2,1,0:T(8,128)(2,1)S(1)}, bf16[96,48,128]{2,1,0:T(8,128)(2,1)}, u32[]{:S(2)}) copy-start(bf16[96,48,128]{2,1,0:T(8,128)(2,1)} %param.20) | copy-start | bytes 3538948
  7.2 6.9 %copy-start.3 = (s32[384]{0:T(512)S(1)}, s32[384]{0:T(512)}, u32[]{:S(2)}) copy-start(s32[384]{0:T(512)} %param.23) | copy-start | bytes 4612
  14.2 31.6 %copy-start.2 = (bf16[128,64]{0,1:T(8,128)(2,1)S(1)}, bf16[128,64]{0,1:T(8,128)(2,1)}, u32[]{:S(2)}) copy-start(bf16[128,64]{0,1:T(8,128)(2,1)} %param.39) | copy-start | bytes 49156
  100.5 49.8 %copy-start.1 = (bf16[96,128]{1,0:T(8,128)(2,1)S(1)}, bf16[96,128]{1,0:T(8,128)(2,1)}, u32[]{:S(2)}) copy-start(bf16[96,128]{1,0:T(8,128)(2,1)} %get-tuple-element.29) | copy-start | bytes 73732

commit v2 on v1

--- a/solution.py
+++ b/solution.py
@@ -229,7 +229,7 @@
 def bias_rows(pair_ref, gain, weight, mixed_ref, out_ref, tr, tc):
     heads = weight.shape[0]
 
-    @pl.loop(0, tc, unroll=4)
+    @pl.loop(0, tc, unroll=12)
     def _(j):
         normed = normalize(pair_ref[pl.ds(j, tr, stride=tc), :], gain).astype(jnp.bfloat16)
         mixed_ref[pl.ds(j * heads, heads), 0:tr] = lax.dot_general(
@@ -288,7 +288,7 @@
         right = jnp.where(low, pltpu.roll(right, channels // 2, axis=1), right)[None]
         gain = transition_ref[pl.ds(layer, 1), :]
 
-        @pl.loop(0, tr // rows)
+        @pl.loop(0, tr // rows, unroll=3)
         def _(step):
             at = pl.ds(pl.multiple_of(step * (rows * tc), rows * tc), rows * tc)
             left = left_ref[pl.ds(pl.multiple_of(step * rows, rows), rows), :][:, None, :]
@@ -353,78 +353,146 @@
 
 
 def mirror(logit_flat, flat, tile_rows, tile_cols, bin_count, own_id):
+    nr, nc = lax.axis_size("row"), lax.axis_size("col")
     parts = tile_rows // tile_cols
     half = tile_cols // 2
-
-    def kernel(flat_ref, logit_ref, final_ref, out_ref, wide_ref, send_sem, recv_sem, local_sem):
+    width = flat.shape[2]
+    depth = flat.shape[1] // nc
+    flat = flat.reshape(parts, nc, depth, width)
+
+    def kernel(
+        flat_ref,
+        logit_ref,
+        final_ref,
+        spread_ref,
+        moved_ref,
+        landed_ref,
+        wide_ref,
+        send_1,
+        send_2,
+        send_3,
+        recv_1,
+        recv_2,
+        recv_3,
+    ):
         row, col = lax.axis_index("row"), lax.axis_index("col")
-        peer_row, slot = lax.div(col, parts), lax.rem(col, parts)
         barrier = pltpu.get_barrier_semaphore()
-        on_diagonal = peer_row == row
-        for part in range(parts):
-            same = jnp.logical_and(on_diagonal, slot == part)
-
-            @pl.when(jnp.logical_not(same))
-            def _(part=part):
+        for axis, total, me in (("col", nc, col), ("row", nr, row)):
+            for step in range(1, total):
                 pl.semaphore_signal(
                     barrier,
                     inc=1,
-                    device_id={"row": peer_row, "col": row * parts + part},
+                    device_id={axis: lax.rem(me + step, total)},
                     device_id_type=MESH,
                 )
-
-        pl.semaphore_wait(barrier, jnp.where(on_diagonal, parts - 1, parts))
-        for part in range(parts):
-            same = jnp.logical_and(on_diagonal, slot == part)
-            away = pltpu.make_async_remote_copy(
-                src_ref=flat_ref.at[part],
-                dst_ref=out_ref.at[slot],
-                send_sem=send_sem.at[part],
-                recv_sem=recv_sem.at[slot],
-                device_id={"row": peer_row, "col": row * parts + part},
+        pl.semaphore_wait(barrier, nc + nr - 2)
+
+        def away(source, target, send, recv, axis, peer):
+            return pltpu.make_async_remote_copy(
+                src_ref=source,
+                dst_ref=target,
+                send_sem=send,
+                recv_sem=recv,
+                device_id={axis: peer},
                 device_id_type=MESH,
             )
-            stay = pltpu.make_async_copy(flat_ref.at[part], out_ref.at[part], local_sem)
-            pl.when(jnp.logical_not(same))(away.start)
+
+        sent = []
+
+        def forward(source, target, send, recv, axis, peer, me):
+            remote = away(source, target, send, recv, axis, peer)
+            stay = pltpu.make_async_copy(source, target, recv)
+            same = peer == me
+            pl.when(jnp.logical_not(same))(remote.start)
             pl.when(same)(stay.start)
-        for part in range(parts):
-            same = jnp.logical_and(on_diagonal, slot == part)
-            away = pltpu.make_async_remote_copy(
-                src_ref=flat_ref.at[part],
-                dst_ref=out_ref.at[part],
-                send_sem=send_sem.at[part],
-                recv_sem=recv_sem.at[part],
-                device_id={"row": peer_row, "col": row * parts + part},
-                device_id_type=MESH,
-            )
-            stay = pltpu.make_async_copy(flat_ref.at[part], out_ref.at[part], local_sem)
-            pl.when(jnp.logical_not(same))(away.wait)
-            pl.when(same)(stay.wait)
-        for part in range(parts):
-            wide_ref[...] = out_ref[part].astype(jnp.float32)
-
-            @pl.loop(0, tile_cols, unroll=4)
-            def _(i, part=part):
+            sent.append((same, remote))
+
+        def arrive(target, recv):
+            pltpu.make_async_copy(target, target, recv).wait()
+
+        for step in range(nc):
+            peer = lax.rem(col + step, nc)
+            for part in range(parts):
+                if step:
+                    remote = away(
+                        flat_ref.at[part, peer],
+                        spread_ref.at[col, part],
+                        send_1.at[step, part],
+                        recv_1.at[col, part],
+                        "col",
+                        peer,
+                    )
+                    remote.start()
+                    sent.append((None, remote))
+        for step in range(nc):
+            origin = lax.rem(col + nc - step, nc)
+            peer, slot = lax.div(origin, parts), lax.rem(origin, parts)
+            for part in range(parts):
+                if step:
+                    arrive(spread_ref.at[origin, part], recv_1.at[origin, part])
+                forward(
+                    spread_ref.at[origin, part] if step else flat_ref.at[part, col],
+                    moved_ref.at[row, slot, part],
+                    send_2.at[step, part],
+                    recv_2.at[row, slot, part],
+                    "row",
+                    peer,
+                    row,
+                )
+        for step in range(nr):
+            origin = lax.rem(row + step, nr)
+            for slot in range(parts):
+                for part in range(parts):
+                    arrive(moved_ref.at[origin, slot, part], recv_2.at[origin, slot, part])
+                    forward(
+                        moved_ref.at[origin, slot, part],
+                        landed_ref.at[col, slot],
+                        send_3.at[step, slot, part],
+                        recv_3.at[col, slot],
+                        "col",
+                        origin * parts + part,
+                        col,
+                    )
+        for slot in range(parts):
+            for piece in range(nc):
+                arrive(landed_ref.at[piece, slot], recv_3.at[piece, slot])
+                wide_ref[piece * depth : (piece + 1) * depth, :] = landed_ref[
+                    piece, slot
+                ].astype(jnp.float32)
+
+            @pl.loop(0, tile_cols, unroll=8)
+            def _(i, slot=slot):
                 packed = wide_ref[pl.ds(i, half, stride=tile_cols), :]
-                other = pltpu.roll(packed, packed.shape[1] - bin_count, axis=1)
+                other = pltpu.roll(packed, width - bin_count, axis=1)
                 flipped = jnp.concatenate([packed, other], axis=0)
-                at = pl.multiple_of((part * tile_cols + i) * tile_cols, 16)
+                at = pl.multiple_of((slot * tile_cols + i) * tile_cols, 16)
                 own = logit_ref[pl.ds(at, tile_cols), :].astype(jnp.float32)
                 final = ((own + flipped) * 0.5).astype(jnp.bfloat16)
-                final_ref[part * tile_cols + i] = final[:, :bin_count]
-
-    width = flat.shape[2]
+                final_ref[slot * tile_cols + i] = final[:, :bin_count]
+
+        for same, remote in sent:
+            if same is None:
+                remote.wait_send()
+            else:
+                pl.when(jnp.logical_not(same))(remote.wait_send)
+
+    dma = pltpu.SemaphoreType.DMA
     return pl.pallas_call(
         kernel,
         out_shape=jax.ShapeDtypeStruct((tile_rows, tile_cols, bin_count), jnp.bfloat16),
         in_specs=[full_spec()] * 2,
         out_specs=full_spec(),
         scratch_shapes=[
-            pltpu.VMEM(flat.shape, flat.dtype),
-            pltpu.VMEM((half * tile_cols, width), jnp.float32),
-            pltpu.SemaphoreType.DMA((parts,)),
-            pltpu.SemaphoreType.DMA((parts,)),
-            pltpu.SemaphoreType.DMA,
+            pltpu.VMEM((nc, parts, depth, width), flat.dtype),
+            pltpu.VMEM((nr, parts, parts, depth, width), flat.dtype),
+            pltpu.VMEM((nc, parts, depth, width), flat.dtype),
+            pltpu.VMEM((nc * depth, width), jnp.float32),
+            dma((nc, parts)),
+            dma((nc, parts)),
+            dma((nr, parts, parts)),
+            dma((nc, parts)),
+            dma((nr, parts, parts)),
+            dma((nc, parts)),
         ],
         compiler_params=pltpu.CompilerParams(collective_id=own_id, has_side_effects=True),
     )(flat, logit_flat)

time: 151 us -> 127 us (0.84)
  the two profiles are of different devices: /device:TPU:3 before, /device:TPU:5 now
where the time goes in v2:
time: 127 us
  Pallas kernels  115 us (91%)
  local copies, waits for them, and re-layouts  5.66 us (4%)
  other arithmetic  4.09 us (3%)
  matrix products  1.51 us (1%)
    pallas_call x2, Pallas kernels, sequence_step(): pl.pallas_call(kernel, out_shape=(jax.ShapeDtypeStruct((tr, width), bf16)...  55.1 us
    pallas_call x1, Pallas kernels, mirror(): pl.pallas_call(kernel, out_shape=jax.ShapeDtypeStruct((tile_rows, tile_co...  30.1 us
    pallas_call x2, Pallas kernels, pair_step(): pl.pallas_call(kernel, out_shape=(jax.ShapeDtypeStruct((tr * tc, width if...  24.6 us
    pallas_call x1, Pallas kernels, bias_step(): pl.pallas_call(kernel, out_shape=jax.ShapeDtypeStruct((heads, tc, lanes),...  5.18 us
    unnamed x11, local copies, waits for them, and re-layouts  3.19 us

profile of v2, /device:TPU:5, one launch (start us, length us, event | category | flops | bytes accessed | tf_op | source)
XLA Modules:
  0.0 127.0 jit_solution(13917193400971967914)
XLA Ops:
  0.6 0.0 copy-start
  0.6 0.9 dynamic-slice_compare_fusion
  1.5 0.8 dynamic_slice.14
  2.3 0.8 dynamic-slice_compare_fusion.1
  3.0 0.8 dynamic_slice.15
  3.8 0.1 add_select_fusion
  3.9 0.1 select_n.22
  4.0 1.5 %fusion = f32[4608,128]{1,0:T(8,128)S(1)} fusion(s32[4608]{0:T(1024)S(1)} %select_n.22, bf16[66,128]{1,0:T(8,128)(2,1)} %param.24), kind=kOutput, calls=%fused_computation.2 | convolution fusion | flops 151584768 | bytes 2394624 | tf_op jit(solution)/shard_map/dot_general | solution.py:540
  5.5 0.0 copy-done
  5.5 1.7 %convert_add_fusion = f32[96,48,128]{2,1,0:T(8,128)} fusion(f32[96,48,128]{2,1,0:T(8,128)S(1)} %bitcast.12, bf16[96,48,128]{2,1,0:T(8,128)(2,1)S(1)} %copy-done), kind=kLoop, calls=%fused_computation.1 | loop fusion | flops 1179648 | bytes 5898240 | tf_op jit(solution)/shard_map/add | solution.py:540
  7.2 0.0 copy-start.3
  7.2 5.2 %shard_map.203.refs_1_ = bf16[32,48,128]{2,1,0:T(8,128)(2,1)} custom-call(f32[4608,128]{1,0:T(8,128)} %bitcast.10, f32[2,128]{1,0:T(2,128)} %bias_gain_ref.3, bf16[2,32,128]{2,1,0:T(8,128)(2,1)} %bitcast.14), custom_call_target="tpu_custom_call" | custom-call | tf_op jit(solution)/shard_map/pallas_call | solution.py:250
  12.4 0.0 copy-done.3
  12.4 0.0 copy-start.2
  12.4 0.8 reshape.71.refs_2_.refs_3_
  13.2 30.8 %shard_map.204 = (bf16[96,128]{1,0:T(8,128)(2,1)}, bf16[8,96,128]{2,1,0:T(8,128)(2,1)}, bf16[4,96,128]{2,1,0:T(8,128)(2,1)}) custom-call(bf16[96,128]{1,0:T(8,128)(2,1)} %refs_0_.1, bf16[32,48,128]{2,1,0:T(8,128)(2,1)} %shard_map.203.refs_1_, s32[384,1]{1,0:T(8,128)} %reshape.71.refs_2_.refs_3_, f32[2,1024]{1,0:T(2,128)} %refs_4_.3, f32[2,1024]{1,0:T(2,128)} %refs_5_.3, ...), custom_call_target="tpu_custom_call" | custom-call | tf_op jit(solution)/shard_map/pallas_call | solution.py:203
  44.0 0.0 copy-done.2
  44.0 0.1 copy.26
  44.1 0.1 pad_bitcast_fusion.1
  44.2 0.7 pad_maximum_fusion.bins_ref
  44.9 13.4 %shard_map.205 = (bf16[4608,128]{1,0:T(8,128)(2,1)}, bf16[32,48,128]{2,1,0:T(8,128)(2,1)}) custom-call(f32[4608,128]{1,0:T(8,128)} %bitcast.11, bf16[384,128]{1,0:T(8,128)(2,1)} %bitcast.17, bf16[2,128,128]{2,1,0:T(8,128)(2,1)} %outer_ref.3, bf16[2,128,512]{2,1,0:T(8,128)(2,1)} %up_ref.3, bf16[2,512,128]{2,1,0:T(8,128)(2,1)} %down_ref.3, ...), custom_call_target="tpu_custom_call" | custom-call | tf_op jit(solution)/shard_map/pallas_call | solution.py:339
  58.2 24.3 %shard_map.206 = (bf16[96,128]{1,0:T(8,128)(2,1)}, bf16[8,96,128]{2,1,0:T(8,128)(2,1)}, bf16[4,96,128]{2,1,0:T(8,128)(2,1)}) custom-call(bf16[96,128]{1,0:T(8,128)(2,1)} %get-tuple-element.13.refs_0_, bf16[8,96,128]{2,1,0:T(8,128)(2,1)} %get-tuple-element.14.refs_1_, bf16[32,48,128]{2,1,0:T(8,128)(2,1)} %get-tuple-element.15.refs_2_, ...), custom_call_target="tpu_custom_call" | custom-call | tf_op jit(solution)/shard_map/pallas_call | solution.py:203
  82.5 11.3 %shard_map.207 = (bf16[4608,128]{1,0:T(8,128)(2,1)}, bf16[2,1152,128]{2,1,0:T(8,128)(2,1)}) custom-call(bf16[4608,128]{1,0:T(8,128)(2,1)} %get-tuple-element.12.pair_ref, bf16[384,128]{1,0:T(8,128)(2,1)} %bitcast.18, bf16[2,128,128]{2,1,0:T(8,128)(2,1)} %outer_ref.3, bf16[2,128,512]{2,1,0:T(8,128)(2,1)} %up_ref.3, bf16[2,512,128]{2,1,0:T(8,128)(2,1)} %down_ref.3, ...), custom_call_target="tpu_custom_call" | custom-call | tf_op jit(solution)/shard_map/pallas_call | solution.py:339
  93.8 0.0 copy-start.1
  93.8 30.1 %shard_map.208 = bf16[96,48,64]{2,1,0:T(8,128)(2,1)} custom-call(bf16[2,8,144,128]{3,2,1,0:T(8,128)(2,1)} %bitcast.13, bf16[4608,128]{1,0:T(8,128)(2,1)} %get-tuple-element.18.logit_ref), custom_call_target="tpu_custom_call" | custom-call | tf_op jit(solution)/shard_map/pallas_call | solution.py:480
  124.0 2.4 %copy.29 = bf16[96,48,64]{0,2,1:T(8,128)(2,1)} copy(bf16[96,48,64]{2,1,0:T(8,128)(2,1)} %shard_map.208) | data formatting | bytes 1179648
  126.4 0.0 copy-done.1
  126.4 0.6 copy.31
Async XLA Ops:
  0.6 4.8 %copy-start = (bf16[96,48,128]{2,1,0:T(8,128)(2,1)S(1)}, bf16[96,48,128]{2,1,0:T(8,128)(2,1)}, u32[]{:S(2)}) copy-start(bf16[96,48,128]{2,1,0:T(8,128)(2,1)} %param.20) | copy-start | bytes 3538948
  7.2 5.2 %copy-start.3 = (s32[384]{0:T(512)S(1)}, s32[384]{0:T(512)}, u32[]{:S(2)}) copy-start(s32[384]{0:T(512)} %param.23) | copy-start | bytes 4612
  12.4 31.6 %copy-start.2 = (bf16[128,64]{0,1:T(8,128)(2,1)S(1)}, bf16[128,64]{0,1:T(8,128)(2,1)}, u32[]{:S(2)}) copy-start(bf16[128,64]{0,1:T(8,128)(2,1)} %param.39) | copy-start | bytes 49156
  93.8 32.6 %copy-start.1 = (bf16[96,128]{1,0:T(8,128)(2,1)S(1)}, bf16[96,128]{1,0:T(8,128)(2,1)}, u32[]{:S(2)}) copy-start(bf16[96,128]{1,0:T(8,128)(2,1)} %get-tuple-element.29) | copy-start | bytes 73732

commit v3 on v2

--- a/solution.py
+++ b/solution.py
@@ -69,9 +69,9 @@
         seq_all_ref = None if first else next(it)
         bias_ref, live_ref, gain_ref, outer_gain_ref = (next(it) for _ in range(4))
         weight_hbm = [next(it) for _ in range(6)]
-        seq_out, seq_out_all, proj_all = (next(it) for _ in range(3))
+        seq_out, seq_out_all, left_out, right_out = (next(it) for _ in range(4))
         weight_refs = [next(it) for _ in range(6)]
-        gathered, kv_all, bias_all, gated_all = (next(it) for _ in range(4))
+        gathered, kv_all, bias_all, gated_all, right_send = (next(it) for _ in range(5))
         weight_sem = next(it)
         col_send, col_recv, row_send, row_recv = (next(it) for _ in range(4))
 
@@ -186,16 +186,32 @@
             lane_join(seq_out_all).astype(jnp.float32), outer_gain_ref[pl.ds(layer, 1), :]
         ).astype(jnp.bfloat16)
         loads[5].wait()
-        proj_all[row] = product(outer_in, 5).astype(jnp.bfloat16)
-        finish(
-            spread(
-                lambda peer: proj_all.at[row],
-                lambda me: proj_all.at[me],
-                "row",
-                row_send.at[1],
-                row_recv.at[1],
-            )
-        )
+        projected = product(outer_in, 5)
+        left_out[...] = projected.astype(jnp.bfloat16)
+        parts = tr // tc
+        holder = lax.div(col, parts)
+        right_send[...] = left_out[pl.ds(pl.multiple_of(lax.rem(col, parts) * tc, 16), tc), :]
+        right_copies = [
+            pltpu.make_async_remote_copy(
+                src_ref=right_send,
+                dst_ref=right_out,
+                send_sem=row_send.at[1, step - 1],
+                recv_sem=row_recv.at[1, 0],
+                device_id={"row": lax.rem(row + step, nr)},
+                device_id_type=MESH,
+            )
+            for step in range(1, nr)
+        ]
+
+        @pl.when(row == holder)
+        def _():
+            for copy in right_copies:
+                copy.start()
+            right_out[...] = right_send[...]
+            for copy in right_copies:
+                copy.wait_send()
+
+        pl.when(row != holder)(right_copies[0].wait_recv)
 
     operands = [seq_tile] + ([] if first else [seq_all]) + [bias_send, live_column, *gains]
     specs = [full_spec()] * len(operands) + [pl.BlockSpec(memory_space=pl.ANY)] * 6
@@ -205,10 +221,11 @@
         out_shape=(
             jax.ShapeDtypeStruct((tr, width), bf16),
             jax.ShapeDtypeStruct((nc, tr, width), bf16),
-            jax.ShapeDtypeStruct((nr, tr, wide), bf16),
+            jax.ShapeDtypeStruct((tr, wide), bf16),
+            jax.ShapeDtypeStruct((tc, wide), bf16),
         ),
         in_specs=specs,
-        out_specs=(full_spec(),) * 3,
+        out_specs=(full_spec(),) * 4,
         scratch_shapes=[pltpu.VMEM((cs, width), bf16)] * 5
         + [
             pltpu.VMEM((cs, wide), bf16),
@@ -216,6 +233,7 @@
             pltpu.VMEM((nr, 2, tr, width), bf16),
             pltpu.VMEM((nc, hl, tc, lanes), bf16),
             pltpu.VMEM((nc, tr, width), bf16),
+            pltpu.VMEM((tc, wide), bf16),
             pltpu.SemaphoreType.DMA((6,)),
             pltpu.SemaphoreType.DMA((4, nc - 1)),
             pltpu.SemaphoreType.DMA((4, nc - 1)),
@@ -256,91 +274,87 @@
     )(pair_flat, bias_norm_gain, bias_weight_t)
 
 
-def pair_step(layer, last, pair_flat, proj_all, tr, tc, mats, gains, bias_weight_t, heads_of_bins):
+def pair_rows(layer, pair_ref, left_ref, right_ref, mats, transition_ref, duplicated_ref, tr, tc):
+    channels = pair_ref.shape[1]
+    rows = 8
+    outer_ref, up_ref, down_ref = mats
+    low = lax.broadcasted_iota(jnp.int32, (1, channels), 1) < channels // 2
+    left = left_ref[...].astype(jnp.float32)
+    duplicated_ref[...] = jnp.where(low, left, pltpu.roll(left, channels // 2, axis=1))
+    right = right_ref[...].astype(jnp.float32)
+    right = jnp.where(low, pltpu.roll(right, channels // 2, axis=1), right)[None]
+    gain = transition_ref[pl.ds(layer, 1), :]
+
+    def update(first, last, store):
+        @pl.loop(first // rows, last // rows, unroll=3)
+        def _(step):
+            at = pl.ds(pl.multiple_of(step * (rows * tc), rows * tc), rows * tc)
+            left = duplicated_ref[pl.ds(pl.multiple_of(step * rows, rows), rows), :][:, None, :]
+            features = jnp.where(low[None], left * right, left - right)
+            features = features.reshape(rows * tc, channels).astype(jnp.bfloat16)
+            middle = pair_ref[at, :].astype(jnp.float32) + jnp.dot(
+                features, outer_ref[layer], preferred_element_type=jnp.float32
+            )
+            normed = normalize(middle, gain).astype(jnp.bfloat16)
+            hidden = jnp.maximum(
+                jnp.dot(normed, up_ref[layer], preferred_element_type=jnp.float32), 0.0
+            ).astype(jnp.bfloat16)
+            store(
+                at,
+                (
+                    middle + jnp.dot(hidden, down_ref[layer], preferred_element_type=jnp.float32)
+                ).astype(jnp.bfloat16),
+            )
+
+    return update
+
+
+def pair_step(layer, pair_flat, left, right, tr, tc, mats, gains, bias_weight_t):
     channels = pair_flat.shape[1]
     heads = bias_weight_t.shape[1]
     lanes = (tr + 127) // 128 * 128
-    rows = 8
-    parts = tr // tc
-    half = tc // 2
 
     def kernel(
         pair_ref,
-        proj_ref,
+        left_ref,
+        right_ref,
         outer_ref,
         up_ref,
         down_ref,
         transition_ref,
         bias_gain_ref,
         bias_weight_ref,
-        bins_ref,
         out_ref,
-        extra_ref,
+        bias_ref,
         fresh_ref,
         mixed_ref,
-        left_ref,
+        duplicated_ref,
     ):
-        row, col = lax.axis_index("row"), lax.axis_index("col")
-        low = lax.broadcasted_iota(jnp.int32, (1, channels), 1) < channels // 2
-        left = proj_ref[pl.ds(pl.multiple_of(row * tr, 16), tr), :].astype(jnp.float32)
-        left_ref[...] = jnp.where(low, left, pltpu.roll(left, channels // 2, axis=1))
-        right = proj_ref[pl.ds(pl.multiple_of(col * tc, 16), tc), :].astype(jnp.float32)
-        right = jnp.where(low, pltpu.roll(right, channels // 2, axis=1), right)[None]
-        gain = transition_ref[pl.ds(layer, 1), :]
-
-        @pl.loop(0, tr // rows, unroll=3)
-        def _(step):
-            at = pl.ds(pl.multiple_of(step * (rows * tc), rows * tc), rows * tc)
-            left = left_ref[pl.ds(pl.multiple_of(step * rows, rows), rows), :][:, None, :]
-            features = jnp.where(low[None], left * right, left - right)
-            features = features.reshape(rows * tc, channels).astype(jnp.bfloat16)
-            middle = pair_ref[at, :].astype(jnp.float32) + jnp.dot(
-                features, outer_ref[layer], preferred_element_type=jnp.float32
-            )
-            normed = normalize(middle, gain).astype(jnp.bfloat16)
-            hidden = jnp.maximum(
-                jnp.dot(normed, up_ref[layer], preferred_element_type=jnp.float32), 0.0
-            ).astype(jnp.bfloat16)
-            fresh = (
-                middle + jnp.dot(hidden, down_ref[layer], preferred_element_type=jnp.float32)
-            ).astype(jnp.bfloat16)
-            if last:
-                fresh_ref[at, :] = fresh.astype(jnp.float32)
-                out_ref[at, :] = jnp.dot(
-                    fresh, bins_ref[0], preferred_element_type=jnp.float32
-                ).astype(jnp.bfloat16)
-            else:
-                out_ref[at, :] = fresh
-                fresh_ref[at, :] = fresh.astype(jnp.float32)
-
-        if last:
-            count = half * tc
-            for part in range(parts):
-                near = fresh_ref[pl.ds(part * 2 * count, count), :].astype(jnp.bfloat16)
-                far = fresh_ref[pl.ds((part * 2 + 1) * count, count), :].astype(jnp.bfloat16)
-                extra_ref[part] = (
-                    jnp.dot(near, bins_ref[0], preferred_element_type=jnp.float32)
-                    + jnp.dot(far, bins_ref[1], preferred_element_type=jnp.float32)
-                ).astype(jnp.bfloat16)
-        else:
-            bias_rows(
-                fresh_ref,
-                bias_gain_ref[pl.ds(layer + 1, 1), :],
-                bias_weight_ref[layer + 1],
-                mixed_ref,
-                extra_ref,
-                tr,
-                tc,
-            )
-
-    width = heads_of_bins.shape[2]
-    extra = (parts, half * tc, width) if last else (heads, tc, lanes)
-    operands = (pair_flat, proj_all, *mats, *gains, bias_weight_t, heads_of_bins)
+        def store(at, fresh):
+            out_ref[at, :] = fresh
+            fresh_ref[at, :] = fresh.astype(jnp.float32)
+
+        mats_refs = (outer_ref, up_ref, down_ref)
+        update = pair_rows(
+            layer, pair_ref, left_ref, right_ref, mats_refs, transition_ref, duplicated_ref, tr, tc
+        )
+        update(0, tr, store)
+        bias_rows(
+            fresh_ref,
+            bias_gain_ref[pl.ds(layer + 1, 1), :],
+            bias_weight_ref[layer + 1],
+            mixed_ref,
+            bias_ref,
+            tr,
+            tc,
+        )
+
+    operands = (pair_flat, left, right, *mats, *gains, bias_weight_t)
     return pl.pallas_call(
         kernel,
         out_shape=(
-            jax.ShapeDtypeStruct((tr * tc, width if last else channels), jnp.bfloat16),
-            jax.ShapeDtypeStruct(extra, jnp.bfloat16),
+            jax.ShapeDtypeStruct((tr * tc, channels), jnp.bfloat16),
+            jax.ShapeDtypeStruct((heads, tc, lanes), jnp.bfloat16),
         ),
         in_specs=[full_spec()] * len(operands),
         out_specs=(full_spec(),) * 2,
@@ -352,18 +366,30 @@
     )(*operands)
 
 
-def mirror(logit_flat, flat, tile_rows, tile_cols, bin_count, own_id):
+def last_step(layer, pair_flat, left, right, tile_rows, tile_cols, mats, gain, bins_pair, own_id):
     nr, nc = lax.axis_size("row"), lax.axis_size("col")
     parts = tile_rows // tile_cols
     half = tile_cols // 2
-    width = flat.shape[2]
-    depth = flat.shape[1] // nc
-    flat = flat.reshape(parts, nc, depth, width)
+    channels = pair_flat.shape[1]
+    width = bins_pair.shape[2]
+    bin_count = width // 2
+    count = half * tile_cols
+    depth = count // nc
 
     def kernel(
+        pair_ref,
+        left_ref,
+        right_ref,
+        outer_ref,
+        up_ref,
+        down_ref,
+        gain_ref,
+        bins_ref,
+        final_ref,
         flat_ref,
         logit_ref,
-        final_ref,
+        fresh_ref,
+        duplicated_ref,
         spread_ref,
         moved_ref,
         landed_ref,
@@ -387,6 +413,24 @@
                 )
         pl.semaphore_wait(barrier, nc + nr - 2)
 
+        def store(at, fresh):
+            fresh_ref[at, :] = fresh.astype(jnp.float32)
+            logit_ref[at, :] = jnp.dot(
+                fresh, bins_ref[0], preferred_element_type=jnp.float32
+            ).astype(jnp.bfloat16)
+
+        update = pair_rows(
+            layer,
+            pair_ref,
+            left_ref,
+            right_ref,
+            (outer_ref, up_ref, down_ref),
+            gain_ref,
+            duplicated_ref,
+            tile_rows,
+            tile_cols,
+        )
+
         def away(source, target, send, recv, axis, peer):
             return pltpu.make_async_remote_copy(
                 src_ref=source,
@@ -410,24 +454,33 @@
         def arrive(target, recv):
             pltpu.make_async_copy(target, target, recv).wait()
 
-        for step in range(nc):
-            peer = lax.rem(col + step, nc)
-            for part in range(parts):
-                if step:
-                    remote = away(
-                        flat_ref.at[part, peer],
-                        spread_ref.at[col, part],
-                        send_1.at[step, part],
-                        recv_1.at[col, part],
-                        "col",
-                        peer,
-                    )
-                    remote.start()
-                    sent.append((None, remote))
-        for step in range(nc):
-            origin = lax.rem(col + nc - step, nc)
-            peer, slot = lax.div(origin, parts), lax.rem(origin, parts)
-            for part in range(parts):
+        for part in range(parts):
+            update(part * tile_cols, (part + 1) * tile_cols, store)
+            near = fresh_ref[pl.ds(part * 2 * count, count), :].astype(jnp.bfloat16)
+            far = fresh_ref[pl.ds((part * 2 + 1) * count, count), :].astype(jnp.bfloat16)
+            packed = jnp.dot(near, bins_ref[0], preferred_element_type=jnp.float32) + jnp.dot(
+                far, bins_ref[1], preferred_element_type=jnp.float32
+            )
+            for piece in range(nc):
+                flat_ref[part, piece] = packed[piece * depth : (piece + 1) * depth].astype(
+                    jnp.bfloat16
+                )
+            for step in range(1, nc):
+                peer = lax.rem(col + step, nc)
+                remote = away(
+                    flat_ref.at[part, peer],
+                    spread_ref.at[col, part],
+                    send_1.at[step, part],
+                    recv_1.at[col, part],
+                    "col",
+                    peer,
+                )
+                remote.start()
+                sent.append((None, remote))
+        for part in range(parts):
+            for step in range(nc):
+                origin = lax.rem(col + nc - step, nc)
+                peer, slot = lax.div(origin, parts), lax.rem(origin, parts)
                 if step:
                     arrive(spread_ref.at[origin, part], recv_1.at[origin, part])
                 forward(
@@ -476,16 +529,22 @@
             else:
                 pl.when(jnp.logical_not(same))(remote.wait_send)
 
+    operands = (pair_flat, left, right, *mats, gain, bins_pair)
+    bf16 = jnp.bfloat16
     dma = pltpu.SemaphoreType.DMA
     return pl.pallas_call(
         kernel,
         out_shape=jax.ShapeDtypeStruct((tile_rows, tile_cols, bin_count), jnp.bfloat16),
-        in_specs=[full_spec()] * 2,
+        in_specs=[full_spec()] * len(operands),
         out_specs=full_spec(),
         scratch_shapes=[
-            pltpu.VMEM((nc, parts, depth, width), flat.dtype),
-            pltpu.VMEM((nr, parts, parts, depth, width), flat.dtype),
-            pltpu.VMEM((nc, parts, depth, width), flat.dtype),
+            pltpu.VMEM((parts, nc, depth, width), bf16),
+            pltpu.VMEM((tile_rows * tile_cols, width), bf16),
+            pltpu.VMEM((tile_rows * tile_cols, channels), jnp.float32),
+            pltpu.VMEM((tile_rows, channels), jnp.float32),
+            pltpu.VMEM((nc, parts, depth, width), bf16),
+            pltpu.VMEM((nr, parts, parts, depth, width), bf16),
+            pltpu.VMEM((nc, parts, depth, width), bf16),
             pltpu.VMEM((nc * depth, width), jnp.float32),
             dma((nc, parts)),
             dma((nc, parts)),
@@ -495,7 +554,7 @@
             dma((nc, parts)),
         ],
         compiler_params=pltpu.CompilerParams(collective_id=own_id, has_side_effects=True),
-    )(flat, logit_flat)
+    )(*operands)
 
 
 def per_device(
@@ -525,12 +584,12 @@
     length = tile_cols * col_total
     row_first = lax.axis_index("row") * tile_rows
     col_first = lax.axis_index("col") * tile_cols
-    row_pos = lax.dynamic_slice_in_dim(residue_index, row_first, tile_rows)
-    col_pos = lax.dynamic_slice_in_dim(residue_index, col_first, tile_cols)
-    row_live = lax.dynamic_slice_in_dim(residue_mask, row_first, tile_rows) > 0
-    col_live = lax.dynamic_slice_in_dim(residue_mask, col_first, tile_cols) > 0
+    coded = jnp.where(residue_mask > 0, residue_index, -1)
+    row_pos = lax.dynamic_slice_in_dim(coded, row_first, tile_rows)
+    col_pos = lax.dynamic_slice_in_dim(coded, col_first, tile_cols)
     offset = jnp.clip(col_pos[None, :] - row_pos[:, None], -RELPOS_MAX, RELPOS_MAX) + RELPOS_MAX + 1
-    bin_index = jnp.where(row_live[:, None] & col_live[None, :], offset, 0)
+    both_live = (row_pos[:, None] >= 0) & (col_pos[None, :] >= 0)
+    bin_index = jnp.where(both_live, offset, 0)
     table_rows = position_table.shape[0]
     padded_rows = (table_rows + 127) // 128 * 128
     table_padded = jnp.pad(position_table, ((0, padded_rows - table_rows), (0, 0)))
@@ -554,7 +613,7 @@
     extra = bias_step(0, pair_flat, tile_rows, tile_cols, bias_norm_gain, bias_weight_t)
     seq_now, seq_all = seq_state, None
     for layer in range(layers):
-        seq_now, seq_all, proj_all = sequence_step(
+        seq_now, seq_all, left, right = sequence_step(
             layer,
             seq_now,
             seq_all,
@@ -565,19 +624,31 @@
             outer_weight,
             layer,
         )
-        pair_flat, extra = pair_step(
-            layer,
-            layer == layers - 1,
-            pair_flat,
-            proj_all.reshape(-1, proj_all.shape[2]),
-            tile_rows,
-            tile_cols,
-            (outer_out_weight, up_weight, down_weight),
-            (transition_gain, bias_norm_gain),
-            bias_weight_t,
-            bins_pair,
-        )
-    distogram = mirror(pair_flat, extra, tile_rows, tile_cols, bin_count, layers)
+        mats = (outer_out_weight, up_weight, down_weight)
+        if layer < layers - 1:
+            pair_flat, extra = pair_step(
+                layer,
+                pair_flat,
+                left,
+                right,
+                tile_rows,
+                tile_cols,
+                mats,
+                (transition_gain, bias_norm_gain),
+                bias_weight_t,
+            )
+    distogram = last_step(
+        layers - 1,
+        pair_flat,
+        left,
+        right,
+        tile_rows,
+        tile_cols,
+        mats,
+        transition_gain,
+        bins_pair,
+        layers,
+    )
     return (distogram, seq_now)
 
 

time: 127 us -> 119 us (0.937)
  the two profiles are of different devices: /device:TPU:5 before, /device:TPU:3 now
where the time goes in v3:
time: 119 us; the launch traced here: 117 us
  Pallas kernels  107 us (90%)
  local copies, waits for them, and re-layouts  4.15 us (3%)
  other arithmetic  3.42 us (3%)
  matrix products  1.51 us (1%)
    pallas_call x2, Pallas kernels, sequence_step(): pl.pallas_call(kernel, out_shape=(jax.ShapeDtypeStruct((tr, width), bf16)...  53.1 us
    pallas_call x1, Pallas kernels, last_step(): pl.pallas_call(kernel, out_shape=jax.ShapeDtypeStruct((tile_rows, tile_co...  35.4 us
    pallas_call x1, Pallas kernels, pair_step(): pl.pallas_call(kernel, out_shape=(jax.ShapeDtypeStruct((tr * tc, channels...  13.3 us
    pallas_call x1, Pallas kernels, bias_step(): pl.pallas_call(kernel, out_shape=jax.ShapeDtypeStruct((heads, tc, lanes),...  5.18 us
    unnamed x11, local copies, waits for them, and re-layouts  3.19 us

profile of v3, /device:TPU:3, one launch (start us, length us, event | category | flops | bytes accessed | tf_op | source)
XLA Modules:
  0.0 116.8 jit_solution(9656457579083795430)
XLA Ops:
  0.6 0.0 copy-start
  0.6 0.8 compare_select_fusion
  1.4 0.1 broadcast_compare_fusion
  1.5 0.1 broadcast_compare_fusion.1
  1.6 0.1 add_select_fusion
  1.7 0.1 select_n.25
  1.8 1.5 %fusion = f32[4608,128]{1,0:T(8,128)S(1)} fusion(s32[4608]{0:T(1024)S(1)} %select_n.25, bf16[66,128]{1,0:T(8,128)(2,1)} %param.24), kind=kOutput, calls=%fused_computation.2 | convolution fusion | flops 151584768 | bytes 2394624 | tf_op jit(solution)/shard_map/dot_general | solution.py:599
  3.3 0.0 copy-done
  3.3 1.7 %convert_add_fusion = f32[96,48,128]{2,1,0:T(8,128)} fusion(f32[96,48,128]{2,1,0:T(8,128)S(1)} %bitcast.9, bf16[96,48,128]{2,1,0:T(8,128)(2,1)S(1)} %copy-done), kind=kLoop, calls=%fused_computation.1 | loop fusion | flops 1179648 | bytes 5898240 | tf_op jit(solution)/shard_map/add | solution.py:599
  5.0 0.0 copy-start.3
  5.0 5.2 %shard_map.203.refs_1_ = bf16[32,48,128]{2,1,0:T(8,128)(2,1)} custom-call(f32[4608,128]{1,0:T(8,128)} %bitcast.7, f32[2,128]{1,0:T(2,128)} %bias_gain_ref.1, bf16[2,32,128]{2,1,0:T(8,128)(2,1)} %bitcast.10), custom_call_target="tpu_custom_call" | custom-call | tf_op jit(solution)/shard_map/pallas_call | solution.py:268
  10.2 0.0 copy-done.3
  10.2 0.8 reshape.61.refs_2_.refs_3_
  11.0 28.9 %shard_map.204 = (bf16[96,128]{1,0:T(8,128)(2,1)}, bf16[8,96,128]{2,1,0:T(8,128)(2,1)}, bf16[96,128]{1,0:T(8,128)(2,1)}, bf16[48,128]{1,0:T(8,128)(2,1)}) custom-call(bf16[96,128]{1,0:T(8,128)(2,1)} %refs_0_.1, bf16[32,48,128]{2,1,0:T(8,128)(2,1)} %shard_map.203.refs_1_, s32[384,1]{1,0:T(8,128)} %reshape.61.refs_2_.refs_3_, f32[2,1024]{1,0:T(2,128)} %refs_4_.3, ...), custom_call_target="tpu_custom_call" | custom-call | tf_op jit(solution)/shard_map/pallas_call | solution.py:219
  39.9 13.3 %shard_map.205 = (bf16[4608,128]{1,0:T(8,128)(2,1)}, bf16[32,48,128]{2,1,0:T(8,128)(2,1)}) custom-call(f32[4608,128]{1,0:T(8,128)} %bitcast.8, bf16[96,128]{1,0:T(8,128)(2,1)} %get-tuple-element.11.left_ref, bf16[48,128]{1,0:T(8,128)(2,1)} %get-tuple-element.12.right_ref, bf16[2,128,128]{2,1,0:T(8,128)(2,1)} %outer_ref.3, bf16[2,128,512]{2,1,0:T(8,128)(2,1)} %up_ref.3, ...), custom_call_target="tpu_custom_call" | custom-call | tf_op jit(solution)/shard_map/pallas_call | solution.py:353
  53.2 0.0 copy-start.2
  53.2 24.2 %shard_map.206 = (bf16[96,128]{1,0:T(8,128)(2,1)}, bf16[8,96,128]{2,1,0:T(8,128)(2,1)}, bf16[96,128]{1,0:T(8,128)(2,1)}, bf16[48,128]{1,0:T(8,128)(2,1)}) custom-call(bf16[96,128]{1,0:T(8,128)(2,1)} %get-tuple-element.14.refs_0_, bf16[8,96,128]{2,1,0:T(8,128)(2,1)} %get-tuple-element.15.refs_1_, bf16[32,48,128]{2,1,0:T(8,128)(2,1)} %get-tuple-element.16.refs_2_, ...), custom_call_target="tpu_custom_call" | custom-call | tf_op jit(solution)/shard_map/pallas_call | solution.py:219
  77.5 0.0 copy-done.2
  77.5 0.1 copy.27
  77.6 0.1 pad_bitcast_fusion.1
  77.7 0.6 pad_maximum_fusion.bins_ref
  78.4 0.0 copy-start.1
  78.4 35.4 %shard_map.207 = bf16[96,48,64]{2,1,0:T(8,128)(2,1)} custom-call(bf16[4608,128]{1,0:T(8,128)(2,1)} %get-tuple-element.13.pair_ref, bf16[96,128]{1,0:T(8,128)(2,1)} %get-tuple-element.17.left_ref, bf16[48,128]{1,0:T(8,128)(2,1)} %get-tuple-element.18.right_ref, bf16[2,128,128]{2,1,0:T(8,128)(2,1)} %outer_ref.3, bf16[2,128,512]{2,1,0:T(8,128)(2,1)} %up_ref.3, ...), custom_call_target="tpu_custom_call" | custom-call | tf_op jit(solution)/shard_map/pallas_call | solution.py:535
  113.8 2.4 %copy.29 = bf16[96,48,64]{0,2,1:T(8,128)(2,1)} copy(bf16[96,48,64]{2,1,0:T(8,128)(2,1)} %shard_map.207) | data formatting | bytes 1179648
  116.2 0.0 copy-done.1
  116.2 0.6 copy.31
Async XLA Ops:
  0.6 2.7 %copy-start = (bf16[96,48,128]{2,1,0:T(8,128)(2,1)S(1)}, bf16[96,48,128]{2,1,0:T(8,128)(2,1)}, u32[]{:S(2)}) copy-start(bf16[96,48,128]{2,1,0:T(8,128)(2,1)} %param.20) | copy-start | bytes 3538948
  5.0 5.2 %copy-start.3 = (s32[384]{0:T(512)S(1)}, s32[384]{0:T(512)}, u32[]{:S(2)}) copy-start(s32[384]{0:T(512)} %param.23) | copy-start | bytes 4612
  53.2 24.3 %copy-start.2 = (bf16[128,64]{0,1:T(8,128)(2,1)S(1)}, bf16[128,64]{0,1:T(8,128)(2,1)}, u32[]{:S(2)}) copy-start(bf16[128,64]{0,1:T(8,128)(2,1)} %param.39) | copy-start | bytes 49156
  78.4 37.9 %copy-start.1 = (bf16[96,128]{1,0:T(8,128)(2,1)S(1)}, bf16[96,128]{1,0:T(8,128)(2,1)}, u32[]{:S(2)}) copy-start(bf16[96,128]{1,0:T(8,128)(2,1)} %get-tuple-element.33) | copy-start | bytes 73732
